TPU v7x, 256 devices: a whole 4x4x8 slice. The times are simulated.
256 devices in a mesh: ka: 32 (over z_lo, y, core), pa: 8 (over z_hi, x).
Axes of the slice: x: 4, y: 4, z: 8 (z_hi: 2, z_lo: 4; z = z_hi * 4 + z_lo), core: 2. Of those that a mesh axis runs over, the one named last changes fastest.
Arguments:
- previous: float32 [256, 256, 256], P('ka', None, 'pa'), may hold values from -6 to 6
- current: float32 [256, 256, 256], P('ka', None, 'pa'), may hold values from -6 to 6
- energies: float32 [256, 256, 256], P('ka', None, 'pa'), may hold values from -0.5 to 0.5
- valence: float32 [256, 256, 256], P('ka'), may hold values from -0.375 to 0.375
- conduction: float32 [256, 256, 256], P('ka', None, 'pa'), may hold values from -0.375 to 0.375
- kernel: float32 [256, 256, 256], P(None, 'ka', 'pa'), may hold values from 0.05 to 0.35
Outputs:
- next_one: float32 [256, 256, 256], P('ka', None, 'pa')
- next_two: float32 [256, 256, 256], P('ka', None, 'pa')
All inputs are finite; a program needn't handle non-finite values.
Results may differ from a plain program's by a relative error of at most 0.000096.
Values sent between devices are 32-bit elements; how exact they have to be, the bound alone decides.
No kernel may reach another device: no remote copies, remote signals or barrier semaphores. Data moves between devices by JAX's collectives and lax.ppermute only.
A program may use at most 64 MiB of HBM per device.

v0:
```python
import math

import jax
import jax.numpy as jnp
from jax import lax
from jax.sharding import PartitionSpec as P

KY = 16


def phase_tables(total):
    points = jnp.arange(total)
    wide = total // KY
    coarse = points // KY
    finer = points % KY
    turns = (coarse[:, None] * coarse[None, :] % wide).astype(jnp.float32) / wide
    turns = turns + (finer[:, None] * finer[None, :] % KY).astype(jnp.float32) / KY
    angles = 2.0 * math.pi * turns
    return (jnp.cos(angles), jnp.sin(angles))


def screen_owned(flattened, kernel, cosine_table, sine_table):
    highest = lax.Precision.HIGHEST
    total = kernel.shape[0]
    even = jnp.dot(cosine_table, flattened, precision=highest)
    odd = jnp.dot(sine_table, flattened, precision=highest)
    weights = kernel.reshape(total, kernel.shape[1] * kernel.shape[2])
    return (
        jnp.dot(cosine_table, weights * even, precision=highest)
        + jnp.dot(sine_table, weights * odd, precision=highest)
    ) / total


def kernel_product(field, valence, conduction, kernel, cosine_table, sine_table):
    highest = lax.Precision.HIGHEST
    total = kernel.shape[0]
    inner = jnp.einsum("kvc,kcn->kvn", field, conduction, precision=highest)
    pair_blocks = jnp.einsum("kvm,kvn->kmn", valence, inner, precision=highest)
    owned = lax.all_to_all(pair_blocks, "ka", split_axis=1, concat_axis=0, tiled=True)
    flattened = owned.reshape(total, owned.shape[1] * owned.shape[2])
    screened = screen_owned(flattened, kernel, cosine_table, sine_table).reshape(owned.shape)
    returned = lax.all_to_all(screened, "ka", split_axis=0, concat_axis=1, tiled=True)
    partial_rows = jnp.einsum("kmn,kcn->kmc", returned, conduction, precision=highest)
    return jnp.einsum("kvm,kmc->kvc", valence, partial_rows, precision=highest)


def on_device(previous, current, energies, valence, conduction, kernel):
    cosine_table, sine_table = phase_tables(kernel.shape[0])
    whole_current = lax.all_gather(current, "pa", axis=2, tiled=True)
    folded_term = kernel_product(
        whole_current, valence, conduction, kernel, cosine_table, sine_table
    )
    summed = lax.psum_scatter(folded_term, "pa", scatter_dimension=2, tiled=True)
    next_one = 2.0 * (energies * current + summed) - previous
    whole_next = lax.all_gather(next_one, "pa", axis=2, tiled=True)
    second_term = kernel_product(whole_next, valence, conduction, kernel, cosine_table, sine_table)
    second_sum = lax.psum_scatter(second_term, "pa", scatter_dimension=2, tiled=True)
    next_two = 2.0 * (energies * next_one + second_sum) - current
    return (next_one, next_two)


def solution(mesh):
    placed = (
        P("ka", None, "pa"),
        P("ka", None, "pa"),
        P("ka", None, "pa"),
        P("ka", None, None),
        P("ka", None, "pa"),
        P(None, "ka", "pa"),
    )
    return jax.shard_map(
        on_device,
        mesh=mesh,
        in_specs=placed,
        out_specs=(P("ka", None, "pa"), P("ka", None, "pa")),
        check_vma=False,
    )
```

profile of v0, /device:TPU:32, one launch (start us, length us, event | category | flops | bytes accessed | tf_op | source)
XLA Modules:
  0.0 476.2 jit_solution(5078884266012246509)
XLA Ops:
  7.9 80.3 %all-gather.3.cloned.1.call-done = f32[8,256,256]{1,2,0:T(8,128)} async-done(((f32[8,256,32]{1,2,0:T(8,128)}), f32[8,256,256]{1,2,0:T(8,128)}) %all-gather.3.cloned.1.call-update) | async-done | bytes 2097168 | tf_op jit(solution)/shard_map/all_gather | solution.py:49
  88.2 3.0 fusion.60
  94.1 6.0 %all-to-all-start = ((f32[32,1,2048]{2,1,0:T(1,128)}), f32[32,1,2048]{2,1,0:T(1,128)S(1)}, u32[]{:S(2)}, u32[]{:S(2)}) async-start(f32[32,1,2048]{2,1,0:T(1,128)} %reshape.71), calls=%async_computation | async-start | bytes 524288 | tf_op jit(solution)/shard_map/all_to_all | solution.py:39
  100.7 1.8 copy.34
  102.5 7.7 %all-to-all-done = f32[32,1,2048]{2,1,0:T(1,128)S(1)} async-done(((f32[32,1,2048]{2,1,0:T(1,128)}), f32[32,1,2048]{2,1,0:T(1,128)S(1)}, u32[]{:S(2)}, u32[]{:S(2)}) %all-to-all-start) | async-done | bytes 262176 | tf_op jit(solution)/shard_map/all_to_all | solution.py:39
  113.4 1.5 reshape.67
  115.0 1.6 convolution_multiply_fusion.2
  116.6 1.6 convolution_multiply_fusion.3
  118.1 1.7 fusion.19
  119.8 1.7 fusion.1
  123.1 15.1 %all_to_all.66 = f32[32,1,2048]{2,1,0:T(1,128)S(1)} all-to-all(f32[32,1,2048]{2,1,0:T(1,128)} %reshape.73), channel_id=1, replica_groups=mesh['ka'=32,'pa'=8] {'ka'}, dimensions={0} | all-to-all | bytes 524288 | tf_op jit(solution)/shard_map/all_to_all | solution.py:42
  138.2 2.0 reduce.1
  141.5 1.9 fusion.4
  143.3 3.5 convolution_bitcast_fusion.1
  146.9 90.9 %reduce-scatter.3.cloned.1.call-done = f32[8,256,32]{1,2,0:T(8,128)} async-done(((f32[8,256,256]{1,2,0:T(8,128)}), f32[8,256,32]{1,2,0:T(8,128)}) %reduce-scatter.3.cloned.1.call-update) | async-done | bytes 262160 | tf_op jit(solution)/shard_map/reduce_scatter | solution.py:53
  237.8 1.7 multiply_subtract_fusion.1
  239.6 72.9 %all-gather.5.cloned.1.call-done = f32[8,256,256]{1,2,0:T(8,128)} async-done(((f32[8,256,32]{1,2,0:T(8,128)}), f32[8,256,256]{1,2,0:T(8,128)}) %all-gather.5.cloned.1.call-update) | async-done | bytes 2097168 | tf_op jit(solution)/shard_map/all_gather | solution.py:55
  312.5 3.0 fusion.61
  315.5 2.0 convolution_bitcast_fusion.2
  320.0 16.2 %all_to_all.67 = f32[32,1,2048]{2,1,0:T(1,128)S(1)} all-to-all(f32[32,1,2048]{2,1,0:T(1,128)} %reshape.75), channel_id=1, replica_groups=mesh['ka'=32,'pa'=8] {'ka'}, dimensions={0} | all-to-all | bytes 524288 | tf_op jit(solution)/shard_map/all_to_all | solution.py:39
  336.2 2.0 reduce.2
  340.6 1.6 reshape.69
  342.2 2.5 convolution_multiply_fusion
  344.8 1.6 convolution_multiply_fusion.1
  346.3 1.7 fusion.16
  348.0 2.4 fusion
  352.9 15.2 %all_to_all.68 = f32[32,1,2048]{2,1,0:T(1,128)S(1)} all-to-all(f32[32,1,2048]{2,1,0:T(1,128)} %reshape.77), channel_id=1, replica_groups=mesh['ka'=32,'pa'=8] {'ka'}, dimensions={0} | all-to-all | bytes 524288 | tf_op jit(solution)/shard_map/all_to_all | solution.py:42
  368.1 2.0 reduce.3
  371.4 1.9 fusion.2
  373.2 3.5 convolution_bitcast_fusion
  376.7 90.9 %reduce-scatter.5.cloned.1.call-done = f32[8,256,32]{1,2,0:T(8,128)} async-done(((f32[8,256,256]{1,2,0:T(8,128)}), f32[8,256,32]{1,2,0:T(8,128)}) %reduce-scatter.5.cloned.1.call-update) | async-done | bytes 262160 | tf_op jit(solution)/shard_map/reduce_scatter | solution.py:57
  467.7 1.7 multiply_subtract_fusion
  (46 shorter events, 19.3 us)
Async XLA Ops:
  7.2 84.0 %copy-start = (f32[8,256,256]{2,1,0:T(8,128)S(1)}, f32[8,256,256]{2,1,0:T(8,128)}, u32[]{:S(2)}) copy-start(f32[8,256,256]{2,1,0:T(8,128)} %param.9) | copy-start | bytes 6291460
  7.2 81.1 %all-gather.3.cloned.1.call-start = ((), (), s32[]{:S(2)}) async-start(), calls=%async_computation.6 | async-start | bytes 2359296 | tf_op jit(solution)/shard_map/all_gather | solution.py:49
  94.1 16.0 %all-to-all-start = ((f32[32,1,2048]{2,1,0:T(1,128)}), f32[32,1,2048]{2,1,0:T(1,128)S(1)}, u32[]{:S(2)}, u32[]{:S(2)}) async-start(f32[32,1,2048]{2,1,0:T(1,128)} %reshape.71), calls=%async_computation | async-start | bytes 524288 | tf_op jit(solution)/shard_map/all_to_all | solution.py:39
  100.1 137.7 %reduce-scatter.3.cloned.1.call-start = ((), (), s32[]{:S(2)}) async-start(), calls=%async_computation.7 | async-start | bytes 2359296 | tf_op jit(solution)/shard_map/reduce_scatter | solution.py:53
  112.3 2.7 copy-start.8
  121.9 19.5 %copy-start.1 = (f32[8,256,32]{1,2,0:T(8,128)S(1)}, f32[8,256,32]{1,2,0:T(8,128)}, u32[]{:S(2)}) copy-start(f32[8,256,32]{1,2,0:T(8,128)} %param.10) | copy-start | bytes 786436
  146.8 91.0 %copy-start.2 = (f32[8,256,32]{1,2,0:T(8,128)S(1)}, f32[8,256,32]{1,2,0:T(8,128)}, u32[]{:S(2)}) copy-start(f32[8,256,32]{1,2,0:T(8,128)} %param.7) | copy-start | bytes 786436
  146.8 91.0 %copy-start.5 = (f32[8,256,32]{1,2,0:T(8,128)S(1)}, f32[8,256,32]{1,2,0:T(8,128)}, u32[]{:S(2)}) copy-start(f32[8,256,32]{1,2,0:T(8,128)} %param.8) | copy-start | bytes 786436
  146.8 91.0 %copy-start.7 = (f32[8,256,32]{1,2,0:T(8,128)S(1)}, f32[8,256,32]{1,2,0:T(8,128)}, u32[]{:S(2)}) copy-start(f32[8,256,32]{1,2,0:T(8,128)} %param.6) | copy-start | bytes 786436
  146.8 165.7 %all-gather.5.cloned.1.call-start = ((), (), s32[]{:S(2)}) async-start(), calls=%async_computation.8 | async-start | bytes 2359296 | tf_op jit(solution)/shard_map/all_gather | solution.py:55
  239.5 228.1 %reduce-scatter.5.cloned.1.call-start = ((), (), s32[]{:S(2)}) async-start(), calls=%async_computation.9 | async-start | bytes 2359296 | tf_op jit(solution)/shard_map/reduce_scatter | solution.py:57
  340.6 4.1 copy-start.9
  376.7 91.0 %copy-start.3 = (f32[8,256,32]{1,2,0:T(8,128)S(1)}, f32[8,256,32]{1,2,0:T(8,128)}, u32[]{:S(2)}) copy-start(f32[8,256,32]{1,2,0:T(8,128)} %param.7) | copy-start | bytes 786436
  376.7 91.0 %copy-start.4 = (f32[8,256,32]{1,2,0:T(8,128)S(1)}, f32[8,256,32]{1,2,0:T(8,128)}, u32[]{:S(2)}) copy-start(f32[8,256,32]{1,2,0:T(8,128)} %multiply_subtract_fusion.1) | copy-start | bytes 786436
  376.7 91.0 %copy-start.6 = (f32[8,256,32]{1,2,0:T(8,128)S(1)}, f32[8,256,32]{1,2,0:T(8,128)}, u32[]{:S(2)}) copy-start(f32[8,256,32]{1,2,0:T(8,128)} %param.8) | copy-start | bytes 786436
Sparse Core Ops, SparseCore 0:
  10.6 77.5 all-gather.2
  146.9 90.7 reduce-scatter.2
  241.0 71.4 all-gather.4
  376.9 90.7 reduce-scatter.4
where the time goes:
time: 481 us; the launch traced here: 476 us
  waiting for transfers between devices  343 us (71%)
  blocking collectives  46.5 us (10%)
  matrix products  34.5 us (7%)
  local copies, waits for them, and re-layouts  20.2 us (4%)
  between operations  14.3 us (3%)
  other arithmetic  10.6 us (2%)
  starting transfers between devices  6.67 us (1%)
    reduce_scatter x1, waiting for transfers between devices, on_device(): lax.psum_scatter(second_term, 'pa', scatter_dimension=2, tiled=True)  90.9 us
    reduce_scatter x1, waiting for transfers between devices, on_device(): lax.psum_scatter(folded_term, 'pa', scatter_dimension=2, tiled=True)  90.9 us
    all_gather x1, waiting for transfers between devices, on_device(): whole_current = lax.all_gather(current, 'pa', axis=2, tiled=True)  80.3 us
    all_gather x1, waiting for transfers between devices, on_device(): whole_next = lax.all_gather(next_one, 'pa', axis=2, tiled=True)  72.9 us
    all_to_all x2, blocking collectives, kernel_product(): lax.all_to_all(screened, 'ka', split_axis=0, concat_axis=1, tiled=True)  30.3 us
    all_to_all x1, blocking collectives, kernel_product(): lax.all_to_all(pair_blocks, 'ka', split_axis=1, concat_axis=0, tiled=True)  16.2 us
  transfers between devices with their start and end apart: 5, of which 5 were waited for; matrix products, arithmetic and copies ran while one was open for 0% of the time, Pallas kernels for 0%

commit v1 on v0

v1 whole, which is shorter than its diff:
```python
import math

import jax
import jax.numpy as jnp
import numpy as np
from jax import lax
from jax.sharding import PartitionSpec as P

KY = 16
HIGHEST = lax.Precision.HIGHEST


def real_transform(total):
    wide = total // KY
    points = np.arange(total)
    coarse, finer = points // KY, points % KY
    mirror = (-coarse % wide) * KY + (-finer % KY)
    alone = [q for q in range(total) if mirror[q] == q]
    paired = [q for q in range(total) if q < mirror[q]]
    turns = (coarse[:, None] * coarse[None, :] % wide) / wide
    turns = turns + (finer[:, None] * finer[None, :] % KY) / KY
    angles = 2.0 * math.pi * turns
    cosine, sine = np.cos(angles), np.sin(angles)
    rows = np.concatenate([cosine[alone], cosine[paired], sine[paired]])
    pick = np.zeros((total, total))
    for i, q in enumerate(alone + paired + paired):
        pick[i, q] = 1.0
        pick[i, mirror[q]] = 1.0
    return rows.astype(np.float32), pick.astype(np.float32)


def product(a, b, dims):
    return lax.dot_general(a, b, (dims, ((), ())), precision=HIGHEST)


def on_device(previous, current, energies, valence, conduction, kernel):
    total = kernel.shape[0]
    rows, pick = real_transform(total)
    both = ("ka", "pa")
    current_t = jnp.swapaxes(current, 1, 2)
    base_t = 2.0 * jnp.swapaxes(energies, 1, 2) * current_t - jnp.swapaxes(previous, 1, 2)
    conduction_t = jnp.swapaxes(conduction, 1, 2)
    kernel_t = jnp.transpose(kernel, (1, 2, 0))
    per_k, slim, bands = current_t.shape
    packed = jnp.stack([current_t, conduction_t, base_t, kernel_t], axis=1)
    packed = lax.all_to_all(packed, "pa", split_axis=0, concat_axis=0, tiled=True)
    whole = [packed[:, i].reshape(per_k * slim, bands) for i in range(4)]
    field_t, conduct_t, whole_base_t, weights_t = whole
    val = lax.dynamic_index_in_dim(valence, lax.axis_index("pa"), 0, keepdims=False)
    weights = product(pick, weights_t, ((1,), (1,))) / total

    def exchange(block):
        block = block.reshape(total, 1, block.shape[1])
        block = lax.all_to_all(block, both, split_axis=0, concat_axis=0, tiled=True)
        return block.reshape(total, block.shape[2])

    def applied_t(amplitudes_t):
        inner = product(conduct_t, amplitudes_t, ((1,), (0,)))
        pairs = product(val, inner, ((0,), (1,)))
        owned = exchange(pairs)
        modes = product(rows, owned, ((1,), (0,))) * weights
        screened = exchange(product(rows, modes, ((0,), (0,))))
        partial = product(conduct_t, screened, ((0,), (1,)))
        return product(partial, val, ((1,), (1,)))

    next_t = whole_base_t + 2.0 * applied_t(field_t)
    second_t = applied_t(next_t)
    home = jnp.stack([next_t, second_t]).reshape(2, per_k, slim, bands)
    home = lax.all_to_all(jnp.swapaxes(home, 0, 1), "pa", split_axis=0, concat_axis=0, tiled=True)
    next_one = jnp.swapaxes(home[:, 0], 1, 2)
    second = jnp.swapaxes(home[:, 1], 1, 2)
    next_two = 2.0 * (energies * next_one + second) - current
    return next_one, next_two


def solution(mesh):
    banded = P("ka", None, "pa")
    return jax.shard_map(
        on_device,
        mesh=mesh,
        in_specs=(banded, banded, banded, P("ka", None, None), banded, P(None, "ka", "pa")),
        out_specs=(banded, banded),
        check_vma=False,
    )
```

time: 481 us -> 165 us (0.34)
  waiting for transfers between devices: 343 us -> 57.9 us
  matrix products: 34.5 us -> 7.55 us
  starting transfers between devices: 6.67 us -> 25.6 us
  blocking collectives: 46.5 us -> 64.8 us
  local copies, waits for them, and re-layouts: 20.2 us -> 3.55 us
  between operations: 14.3 us -> 0.85 us
  other arithmetic: 10.6 us -> 4.41 us
    reduce_scatter x2 -> x0, waiting for transfers between devices: 182 us -> none  [the longest x1 90.9 us: on_device(): lax.psum_scatter(second_term, 'pa', scatter_dimension=2, tiled=True)]
    all_gather x2 -> x0, waiting for transfers between devices: 153 us -> none  [the longest x1 80.3 us: on_device(): whole_current = lax.all_gather(current, 'pa', axis=2, tiled=True)]
    all_to_all x1 -> x3, waiting for transfers between devices: 7.65 us -> 57.9 us  [the longest x1 29 us: on_device(): lax.all_to_all(packed, 'pa', split_axis=0, concat_axis=0, tiled=True)]
    dot_general x16 -> x13, matrix products: 34.5 us -> 7.55 us  [product(): return lax.dot_general(a, b, (dims, ((), ())), precision=HIGHEST)]
    all_to_all x1 -> x3, starting transfers between devices: 5.98 us -> 25.6 us  [the longest x2 15.6 us: exchange(): block = lax.all_to_all(block, both, split_axis=0, concat_axis=0, tiled=True)]
    all_to_all x3, blocking collectives: 46.5 us -> 64.8 us  [the longest x2 42.4 us: exchange(): block = lax.all_to_all(block, both, split_axis=0, concat_axis=0, tiled=True)]
    unnamed x28 -> x12, local copies, waits for them, and re-layouts: 8.87 us -> 0.04 us
    all_to_all x4 -> x0, other arithmetic: 7.12 us -> none  [the longest x2 3.93 us: kernel_product(): lax.all_to_all(screened, 'ka', split_axis=0, concat_axis=1, tiled=True)]
  transfers between devices with their start and end apart: 5 -> 3, of which waited for: 5 -> 3; matrix products, arithmetic and copies ran while one was open for 0% -> 1% of each run, Pallas kernels for 0% -> 0%
where the time goes in v1:
time: 165 us
  blocking collectives  64.8 us (39%)
  waiting for transfers between devices  57.9 us (35%)
  starting transfers between devices  25.6 us (16%)
  matrix products  7.55 us (5%)
  other arithmetic  4.41 us (3%)
  local copies, waits for them, and re-layouts  3.55 us (2%)
    all_to_all x2, blocking collectives, exchange(): block = lax.all_to_all(block, both, split_axis=0, concat_axis=0, tiled=True)  42.4 us
    all_to_all x1, waiting for transfers between devices, on_device(): lax.all_to_all(packed, 'pa', split_axis=0, concat_axis=0, tiled=True)  29 us
    all_to_all x2, waiting for transfers between devices, exchange(): block = lax.all_to_all(block, both, split_axis=0, concat_axis=0, tiled=True)  28.8 us
    all_to_all x1, blocking collectives, on_device(): lax.all_to_all(jnp.swapaxes(home, 0, 1), 'pa', split_axis=0, concat_axis=...  22.4 us
    all_to_all x2, starting transfers between devices, exchange(): block = lax.all_to_all(block, both, split_axis=0, concat_axis=0, tiled=True)  15.6 us
    all_to_all x1, starting transfers between devices, on_device(): lax.all_to_all(packed, 'pa', split_axis=0, concat_axis=0, tiled=True)  10 us
    dot_general x13, matrix products, product(): return lax.dot_general(a, b, (dims, ((), ())), precision=HIGHEST)  7.55 us
    another operation x2, other arithmetic, on_device(): packed = jnp.stack([current_t, conduction_t, base_t, kernel_t], axis=1)  3.51 us
  transfers between devices with their start and end apart: 3, of which 3 were waited for; matrix products, arithmetic and copies ran while one was open for 1% of the time, Pallas kernels for 0%

profile of v1, /device:TPU:32, one launch (start us, length us, event | category | flops | bytes accessed | tf_op | source)
XLA Modules:
  0.0 164.7 jit_solution(13144724496826694902)
XLA Ops:
  0.6 0.0 copy-start
  0.6 1.3 fusion.18
  2.0 2.2 %pad_maximum_fusion = f32[8,4,32,256]{3,2,1,0:T(8,128)} fusion(f32[8,1,32,256]{3,2,1,0:T(8,128)} %bitcast.114, f32[8,1,32,256]{3,2,1,0:T(8,128)S(1)} %fusion.18, f32[8,1,32,256]{3,2,1,0:T(8,128)} %bitcast.115, f32[8,1,32,256]{3,2,1,0:T(8,128)} %bitcast.109), kind=kLoop, calls=%fused_computation.10 | loop fusion | flops 786432 | bytes 2097152 | tf_op jit(solution)/shard_map/stack | solution.py:45
  4.2 10.0 %all-to-all-start = ((f32[8,4,32,256]{3,2,1,0:T(8,128)}), f32[8,4,32,256]{3,2,1,0:T(8,128)S(1)}, u32[]{:S(2)}, u32[]{:S(2)}) async-start(f32[8,4,32,256]{3,2,1,0:T(8,128)} %pad_maximum_fusion), calls=%async_computation | async-start | bytes 2097152 | tf_op jit(solution)/shard_map/all_to_all | solution.py:46
  14.2 29.0 %all-to-all-done = f32[8,4,32,256]{3,2,1,0:T(8,128)S(1)} async-done(((f32[8,4,32,256]{3,2,1,0:T(8,128)}), f32[8,4,32,256]{3,2,1,0:T(8,128)S(1)}, u32[]{:S(2)}, u32[]{:S(2)}) %all-to-all-start) | async-done | bytes 1048608 | tf_op jit(solution)/shard_map/all_to_all | solution.py:46
  43.2 0.9 fusion.27
  44.1 0.4 fusion.28
  44.5 0.6 convolution_bitcast_fusion.4
  45.1 1.0 copy.22
  46.1 9.2 %all-to-all-start.1 = ((f32[256,1,256]{2,1,0:T(1,128)}), f32[256,1,256]{2,1,0:T(1,128)S(1)}, u32[]{:S(2)}, u32[]{:S(2)}) async-start(f32[256,1,256]{2,1,0:T(1,128)} %copy.22), calls=%async_computation.1 | async-start | bytes 524288 | tf_op jit(solution)/shard_map/all_to_all | solution.py:54
  55.3 1.4 convolution_multiply_fusion.2
  56.7 13.8 %all-to-all-done.1 = f32[256,1,256]{2,1,0:T(1,128)S(1)} async-done(((f32[256,1,256]{2,1,0:T(1,128)}), f32[256,1,256]{2,1,0:T(1,128)S(1)}, u32[]{:S(2)}, u32[]{:S(2)}) %all-to-all-start.1) | async-done | bytes 262176 | tf_op jit(solution)/shard_map/all_to_all | solution.py:54
  70.5 0.6 convolution_multiply_fusion.3
  71.1 0.6 convolution_bitcast_fusion.3
  71.7 0.3 copy.23
  71.9 21.2 %all_to_all.30 = f32[256,1,256]{2,1,0:T(1,128)S(1)} all-to-all(f32[256,1,256]{2,1,0:T(1,128)S(1)} %copy.23), channel_id=1, replica_groups=mesh['ka'=32,'pa'=8] {'ka','pa'}, dimensions={0} | all-to-all | bytes 524288 | tf_op jit(solution)/shard_map/all_to_all | solution.py:54
  93.2 0.6 fusion.9
  93.8 0.4 fusion
  94.2 0.4 fusion.29
  94.6 0.6 convolution_bitcast_fusion.2
  95.2 0.3 copy.25
  95.5 21.2 %all_to_all.31 = f32[256,1,256]{2,1,0:T(1,128)S(1)} all-to-all(f32[256,1,256]{2,1,0:T(1,128)S(1)} %copy.25), channel_id=1, replica_groups=mesh['ka'=32,'pa'=8] {'ka','pa'}, dimensions={0} | all-to-all | bytes 524288 | tf_op jit(solution)/shard_map/all_to_all | solution.py:54
  116.7 0.6 convolution_multiply_fusion
  117.3 0.6 convolution_bitcast_fusion.1
  117.9 1.0 copy.26
  118.9 6.4 %all-to-all-start.4 = ((f32[256,1,256]{2,1,0:T(1,128)}), f32[256,1,256]{2,1,0:T(1,128)S(1)}, u32[]{:S(2)}, u32[]{:S(2)}) async-start(f32[256,1,256]{2,1,0:T(1,128)} %copy.26), calls=%async_computation.4 | async-start | bytes 524288 | tf_op jit(solution)/shard_map/all_to_all | solution.py:54
  125.3 0.1 copy.24
  125.4 15.0 %all-to-all-done.4 = f32[256,1,256]{2,1,0:T(1,128)S(1)} async-done(((f32[256,1,256]{2,1,0:T(1,128)}), f32[256,1,256]{2,1,0:T(1,128)S(1)}, u32[]{:S(2)}, u32[]{:S(2)}) %all-to-all-start.4) | async-done | bytes 262176 | tf_op jit(solution)/shard_map/all_to_all | solution.py:54
  140.5 0.4 fusion.4
  140.9 0.4 convolution_bitcast_fusion
  141.4 22.4 %all_to_all.32 = f32[8,2,32,256]{3,2,1,0:T(8,128)S(1)} all-to-all(f32[8,2,32,256]{3,2,1,0:T(8,128)S(1)} %copy.27), channel_id=1, replica_groups=mesh['ka'=32,'pa'=8] {'pa'}, dimensions={0} | all-to-all | bytes 1048576 | tf_op jit(solution)/shard_map/all_to_all | solution.py:69
  163.8 0.9 fusion.3
  (13 shorter events, 0.1 us)
Async XLA Ops:
  0.6 43.9 %copy-start = (f32[8,256,256]{2,1,0:T(8,128)S(1)}, f32[8,256,256]{2,1,0:T(8,128)}, u32[]{:S(2)}) copy-start(f32[8,256,256]{2,1,0:T(8,128)} %param.11) | copy-start | bytes 6291460
  4.2 39.1 %all-to-all-start = ((f32[8,4,32,256]{3,2,1,0:T(8,128)}), f32[8,4,32,256]{3,2,1,0:T(8,128)S(1)}, u32[]{:S(2)}, u32[]{:S(2)}) async-start(f32[8,4,32,256]{3,2,1,0:T(8,128)} %pad_maximum_fusion), calls=%async_computation | async-start | bytes 2097152 | tf_op jit(solution)/shard_map/all_to_all | solution.py:46
  44.1 11.2 %copy-start.4 = (f32[8,1,32,256]{3,2,1,0:T(8,128)S(1)}, f32[8,1,32,256]{3,2,1,0:T(8,128)}, u32[]{:S(2)}) copy-start(f32[8,1,32,256]{3,2,1,0:T(8,128)} %get-tuple-element.5) | copy-start | bytes 786436
  44.1 26.4 %copy-start.1 = (f32[256,256]{1,0:T(8,128)S(1)}, f32[256,256]{1,0:T(8,128)}, u32[]{:S(2)}) copy-start(f32[256,256]{1,0:T(8,128)} %constant.22.clone) | copy-start | bytes 786436
  46.1 24.4 %all-to-all-start.1 = ((f32[256,1,256]{2,1,0:T(1,128)}), f32[256,1,256]{2,1,0:T(1,128)S(1)}, u32[]{:S(2)}, u32[]{:S(2)}) async-start(f32[256,1,256]{2,1,0:T(1,128)} %copy.22), calls=%async_computation.1 | async-start | bytes 524288 | tf_op jit(solution)/shard_map/all_to_all | solution.py:54
  56.7 37.1 %copy-start.5 = (f32[8,1,32,256]{3,2,1,0:T(8,128)S(1)}, f32[8,1,32,256]{3,2,1,0:T(8,128)}, u32[]{:S(2)}) copy-start(f32[8,1,32,256]{3,2,1,0:T(8,128)} %get-tuple-element.7) | copy-start | bytes 786436
  118.9 21.6 %all-to-all-start.4 = ((f32[256,1,256]{2,1,0:T(1,128)}), f32[256,1,256]{2,1,0:T(1,128)S(1)}, u32[]{:S(2)}, u32[]{:S(2)}) async-start(f32[256,1,256]{2,1,0:T(1,128)} %copy.26), calls=%async_computation.4 | async-start | bytes 524288 | tf_op jit(solution)/shard_map/all_to_all | solution.py:54
  140.9 22.9 %copy-start.2 = (f32[8,256,32]{1,2,0:T(8,128)S(1)}, f32[8,256,32]{1,2,0:T(8,128)}, u32[]{:S(2)}) copy-start(f32[8,256,32]{1,2,0:T(8,128)} %param.9) | copy-start | bytes 786436
  140.9 22.9 %copy-start.3 = (f32[8,256,32]{1,2,0:T(8,128)S(1)}, f32[8,256,32]{1,2,0:T(8,128)}, u32[]{:S(2)}) copy-start(f32[8,256,32]{1,2,0:T(8,128)} %param.10) | copy-start | bytes 786436

commit v2 on v1

v2 whole, which is shorter than its diff:
```python
import math

import jax
import jax.numpy as jnp
import numpy as np
from jax import lax
from jax.experimental import pallas as pl
from jax.experimental.pallas import tpu as pltpu
from jax.sharding import PartitionSpec as P

KY = 16
LANES = 128
VMEM_BYTES = 16 * 1024 * 1024
F32 = jnp.float32
BF16 = jnp.bfloat16
NN = (((1,), (0,)), ((), ()))
NT = (((1,), (1,)), ((), ()))


def real_transform(total):
    wide = total // KY
    points = np.arange(total)
    coarse, finer = points // KY, points % KY
    mirror = (-coarse % wide) * KY + (-finer % KY)
    alone = [q for q in range(total) if mirror[q] == q]
    paired = [q for q in range(total) if q < mirror[q]]
    turns = (coarse[:, None] * coarse[None, :] % wide) / wide
    turns = turns + (finer[:, None] * finer[None, :] % KY) / KY
    angles = 2.0 * math.pi * turns
    cosine, sine = np.cos(angles), np.sin(angles)
    rows = np.concatenate([cosine[alone], cosine[paired], sine[paired]])
    pick = np.zeros((total, total))
    for i, q in enumerate(alone + paired + paired):
        pick[i, q] = 1.0
        pick[i, mirror[q]] = 1.0
    return rows.astype(np.float32), pick.astype(np.float32)


def split_table(table):
    high = table.astype(BF16)
    return high, (table - high.astype(np.float32)).astype(BF16)


def split(x):
    high = x.astype(BF16)
    return high, (x - high.astype(F32)).astype(BF16)


def dot3(a, b, dims=NN):
    one = lambda p, q: lax.dot_general(p, q, dims, preferred_element_type=F32)
    return one(a[0], b[0]) + (one(a[0], b[1]) + one(a[1], b[0]))


def swap_groups(blocks):
    lane = lax.broadcasted_iota(jnp.int32, blocks[0].shape, 1)
    low = lane < 64
    a, b, c, d = blocks
    turn = lambda x, by: pltpu.roll(x, by, 1)
    a, c = jnp.where(low, a, turn(c, 64)), jnp.where(low, turn(a, 64), c)
    b, d = jnp.where(low, b, turn(d, 64)), jnp.where(low, turn(b, 64), d)
    even = (lane // 32) % 2 == 0
    a, b = jnp.where(even, a, turn(b, 32)), jnp.where(even, turn(a, 96), b)
    c, d = jnp.where(even, c, turn(d, 32)), jnp.where(even, turn(c, 96), d)
    return a, b, c, d


def store_messages(pairs, out_ref):
    for half in range(2):
        for part in range(2):
            blocks = [pairs[(4 * part + i) * 32 : (4 * part + i) * 32 + 32, half * LANES : (half + 1) * LANES] for i in range(4)]
            for p, block in enumerate(swap_groups(blocks)):
                out_ref[pl.ds((half * 4 + p) * 2 + part, 32, stride=16), :] = block


def load_messages(in_ref):
    halves = []
    for half in range(2):
        rows = []
        for part in range(2):
            blocks = [in_ref[pl.ds((half * 4 + p) * 2 + part, 32, stride=16), :] for p in range(4)]
            rows.extend(swap_groups(blocks))
        halves.append(jnp.concatenate(rows, axis=0))
    return jnp.concatenate(halves, axis=1)


def pack_kernel(previous_ref, current_ref, energies_ref, conduction_ref, out_ref):
    current = current_ref[...]
    out_ref[:, 0] = current
    out_ref[:, 1] = conduction_ref[...]
    out_ref[:, 2] = 2.0 * energies_ref[...] * current - previous_ref[...]


def valence_kernel(index_ref, valence_ref, high_ref, low_ref, turned_ref):
    del index_ref
    turned = valence_ref[0].T
    for half in range(2):
        columns = slice(half * LANES, (half + 1) * LANES)
        turned_ref[half] = turned[:, columns]
        for row in range(8):
            high, low = split(turned_ref[half, pl.ds(row, 32, stride=8), :])
            high_ref[row * 32 : row * 32 + 32, columns] = high
            low_ref[row * 32 : row * 32 + 32, columns] = low


def square(ref, which):
    block = ref[:, which]
    return block.reshape(block.shape[0] * block.shape[1], block.shape[2])


def first_pairs_kernel(whole_ref, high_ref, low_ref, out_ref):
    conduct = split(square(whole_ref, 1))
    inner = dot3(conduct, split(square(whole_ref, 0)))
    store_messages(dot3((high_ref[...], low_ref[...]), split(inner), NT), out_ref)


def screen_kernel(owned_ref, rows_high, rows_low, back_high, back_low, weights_ref, out_ref):
    total = weights_ref.shape[0]
    owned = jnp.concatenate([owned_ref[pl.ds(part, total, stride=2), :] for part in range(2)], axis=1)
    modes = dot3((rows_high[...], rows_low[...]), split(owned)) * weights_ref[...]
    screened = dot3((back_high[...], back_low[...]), split(modes))
    for part in range(2):
        out_ref[pl.ds(part, total, stride=2), :] = screened[:, part * LANES : (part + 1) * LANES]


def product_back(screened_ref, conduct, valence):
    partial = dot3(split(load_messages(screened_ref)), conduct)
    return dot3(split(partial.T), valence)


def next_pairs_kernel(screened_ref, whole_ref, high_ref, low_ref, next_ref, out_ref):
    conduct = split(square(whole_ref, 1))
    valence = high_ref[...], low_ref[...]
    following = square(whole_ref, 2) + 2.0 * product_back(screened_ref, conduct, valence)
    next_ref[...] = following
    inner = dot3(conduct, split(following))
    store_messages(dot3(valence, split(inner), NT), out_ref)


def last_kernel(screened_ref, whole_ref, high_ref, low_ref, next_ref, out_ref):
    conduct = split(square(whole_ref, 1))
    second = product_back(screened_ref, conduct, (high_ref[...], low_ref[...]))
    shape = out_ref.shape[0], out_ref.shape[2], out_ref.shape[3]
    out_ref[:, 0] = next_ref[...].reshape(shape)
    out_ref[:, 1] = second.reshape(shape)


def call(kernel, outs, flops, moved, **more):
    return pl.pallas_call(
        kernel,
        out_shape=outs,
        compiler_params=pltpu.CompilerParams(vmem_limit_bytes=VMEM_BYTES),
        cost_estimate=pl.CostEstimate(flops=flops, bytes_accessed=moved, transcendentals=0),
        **more,
    )


def on_device(previous, current, energies, valence, conduction, kernel):
    total = kernel.shape[0]
    rows, pick = real_transform(total)
    both = ("ka", "pa")
    banded = lambda x: jnp.swapaxes(x, 1, 2)
    per_k, bands, slim = current.shape
    flops = 2 * total**3
    size = 4 * total**2
    shaped = jax.ShapeDtypeStruct
    tables = [jnp.asarray(t) for t in (*split_table(rows), *split_table(rows.T.copy()))]

    packed = call(pack_kernel, shaped((per_k, 3, slim, bands), F32), 3 * total**2, 7 * size)(
        banded(previous), banded(current), banded(energies), banded(conduction)
    )
    whole = lax.all_to_all(packed, "pa", split_axis=0, concat_axis=0, tiled=True)

    high, low = call(
        valence_kernel,
        [shaped((total, bands), BF16)] * 2,
        total**2,
        2 * size,
        grid_spec=pltpu.PrefetchScalarGridSpec(
            num_scalar_prefetch=1,
            grid=(1,),
            in_specs=[pl.BlockSpec((1, bands, total), lambda i, index: (index[0], 0, 0))],
            out_specs=[pl.BlockSpec((total, bands), lambda i, index: (0, 0))] * 2,
            scratch_shapes=[pltpu.VMEM((2, total, LANES), F32)],
        ),
    )(lax.axis_index("pa").reshape(1), valence)
    kernel_t = jnp.transpose(kernel, (1, 2, 0)).reshape(total, total)
    weights = lax.dot_general(pick, kernel_t, NT, precision=lax.Precision.HIGHEST) / total

    def exchange(block):
        block = block.reshape(total, 2, LANES)
        block = lax.all_to_all(block, both, split_axis=0, concat_axis=0, tiled=True)
        return block.reshape(2 * total, LANES)

    message = shaped((2 * total, LANES), F32)
    screen = call(screen_kernel, message, 6 * flops, 5 * size)

    pairs = call(first_pairs_kernel, message, 6 * flops, 4 * size)(whole, high, low)
    back = exchange(screen(exchange(pairs), *tables, weights))
    following, pairs = call(next_pairs_kernel, [shaped((total, bands), F32), message], 12 * flops, 6 * size)(
        back, whole, high, low
    )
    back = exchange(screen(exchange(pairs), *tables, weights))
    home = call(last_kernel, shaped((per_k, 2, slim, bands), F32), 6 * flops, 6 * size)(
        back, whole, high, low, following
    )
    home = lax.all_to_all(home, "pa", split_axis=0, concat_axis=0, tiled=True)
    next_one = banded(home[:, 0])
    next_two = 2.0 * (energies * next_one + banded(home[:, 1])) - current
    return next_one, next_two


def solution(mesh):
    banded = P("ka", None, "pa")
    return jax.shard_map(
        on_device,
        mesh=mesh,
        in_specs=(banded, banded, banded, P("ka", None, None), banded, P(None, "ka", "pa")),
        out_specs=(banded, banded),
        check_vma=False,
    )
```

time: 165 us -> 158 us (0.958)
  waiting for transfers between devices: 57.9 us -> 36.4 us
  blocking collectives: 64.8 us -> 86 us
  starting transfers between devices: 25.6 us -> 18.5 us
  Pallas kernels: 0 us -> 6.51 us
  matrix products: 7.55 us -> 1.36 us
  local copies, waits for them, and re-layouts: 3.55 us -> 7.12 us
  other arithmetic: 4.41 us -> 0.87 us
    all_to_all x2 -> x3, blocking collectives: 42.4 us -> 63.7 us  [exchange(): block = lax.all_to_all(block, both, split_axis=0, concat_axis=0, tiled=True)]
    all_to_all x2 -> x1, waiting for transfers between devices: 28.8 us -> 13.8 us  [exchange(): block = lax.all_to_all(block, both, split_axis=0, concat_axis=0, tiled=True)]
    all_to_all x2 -> x1, starting transfers between devices: 15.6 us -> 8.5 us  [exchange(): block = lax.all_to_all(block, both, split_axis=0, concat_axis=0, tiled=True)]
    unnamed x12 -> x36, local copies, waits for them, and re-layouts: 0.04 us -> 7.12 us
    pallas_call x0 -> x7, Pallas kernels: none -> 6.51 us  [the longest x1 1.66 us: on_device(): call(next_pairs_kernel, [shaped((total, bands), F32), message], 12 * flop...]
    all_to_all x1, waiting for transfers between devices: 29 us -> 22.6 us  [on_device(): lax.all_to_all(packed, 'pa', split_axis=0, concat_axis=0, tiled=True)]
    dot_general x13 -> x1, matrix products: 7.55 us -> 1.36 us  [on_device(): lax.dot_general(pick, kernel_t, NT, precision=lax.Precision.HIGHEST) / total]
    another operation x2 -> x0, other arithmetic: 3.51 us -> none  [on_device(): packed = jnp.stack([current_t, conduction_t, base_t, kernel_t], axis=1)]
  transfers between devices with their start and end apart: 3 -> 2, of which waited for: 3 -> 2; matrix products, arithmetic and copies ran while one was open for 1% -> 1% of each run, Pallas kernels for 0% -> 0%
where the time goes in v2:
time: 158 us
  blocking collectives  86 us (54%)
  waiting for transfers between devices  36.4 us (23%)
  starting transfers between devices  18.5 us (12%)
  local copies, waits for them, and re-layouts  7.12 us (5%)
  Pallas kernels  6.51 us (4%)
    all_to_all x3, blocking collectives, exchange(): block = lax.all_to_all(block, both, split_axis=0, concat_axis=0, tiled=True)  63.7 us
    all_to_all x1, waiting for transfers between devices, on_device(): lax.all_to_all(packed, 'pa', split_axis=0, concat_axis=0, tiled=True)  22.6 us
    all_to_all x1, blocking collectives, on_device(): home = lax.all_to_all(home, 'pa', split_axis=0, concat_axis=0, tiled=True)  22.3 us
    all_to_all x1, waiting for transfers between devices, exchange(): block = lax.all_to_all(block, both, split_axis=0, concat_axis=0, tiled=True)  13.8 us
    all_to_all x1, starting transfers between devices, on_device(): lax.all_to_all(packed, 'pa', split_axis=0, concat_axis=0, tiled=True)  10 us
    all_to_all x1, starting transfers between devices, exchange(): block = lax.all_to_all(block, both, split_axis=0, concat_axis=0, tiled=True)  8.5 us
    unnamed x36, local copies, waits for them, and re-layouts  7.12 us
  transfers between devices with their start and end apart: 2, of which 2 were waited for; matrix products, arithmetic and copies ran while one was open for 1% of the time, Pallas kernels for 0%

profile of v2, /device:TPU:32, one launch (start us, length us, event | category | flops | bytes accessed | tf_op | source)
XLA Modules:
  0.0 157.6 jit_solution(665566037734896478)
XLA Ops:
  0.6 0.0 copy-start
  0.7 0.0 copy-start.2
  0.7 1.1 copy-done.2
  1.8 0.9 copy-done.4
  2.7 0.9 copy-done.16
  3.7 0.9 copy-done.17
  4.6 0.9 shard_map.122
  5.6 10.0 %all-to-all-start = ((f32[8,3,32,256]{3,2,1,0:T(8,128)}), f32[8,3,32,256]{3,2,1,0:T(8,128)S(1)}, u32[]{:S(2)}, u32[]{:S(2)}) async-start(f32[8,3,32,256]{3,2,1,0:T(8,128)} %shard_map.122), calls=%async_computation | async-start | bytes 1572864 | tf_op jit(solution)/shard_map/all_to_all | solution.py:171
  15.6 0.0 copy-start.6
  15.6 0.0 copy-start.7
  15.6 0.0 copy-start.8
  15.6 0.2 shard_map.123
  15.8 0.0 copy-start.10
  15.8 0.6 copy-done.10
  16.5 0.7 copy-done.13
  17.1 22.6 %all-to-all-done.whole_ref = f32[8,3,32,256]{3,2,1,0:T(8,128)S(1)} async-done(((f32[8,3,32,256]{3,2,1,0:T(8,128)}), f32[8,3,32,256]{3,2,1,0:T(8,128)S(1)}, u32[]{:S(2)}, u32[]{:S(2)}) %all-to-all-start) | async-done | bytes 786464 | tf_op jit(solution)/shard_map/all_to_all | solution.py:171
  39.7 0.9 copy-done.11
  40.6 0.9 copy-done.14
  41.5 1.5 shard_map.124
  43.1 8.5 %all-to-all-start.1 = ((f32[256,2,128]{2,1,0:T(2,128)}), f32[256,2,128]{2,1,0:T(2,128)S(1)}, u32[]{:S(2)}, u32[]{:S(2)}) async-start(f32[256,2,128]{2,1,0:T(2,128)} %bitcast.5), calls=%async_computation.1 | async-start | bytes 524288 | tf_op jit(solution)/shard_map/all_to_all | solution.py:191
  51.6 1.4 convolution_multiply_fusion.weights_ref
  52.9 13.8 %all-to-all-done.1 = f32[256,2,128]{2,1,0:T(2,128)S(1)} async-done(((f32[256,2,128]{2,1,0:T(2,128)}), f32[256,2,128]{2,1,0:T(2,128)S(1)}, u32[]{:S(2)}, u32[]{:S(2)}) %all-to-all-start.1) | async-done | bytes 262176 | tf_op jit(solution)/shard_map/all_to_all | solution.py:191
  66.8 0.7 shard_map.125
  67.4 21.2 %all_to_all.30 = f32[256,2,128]{2,1,0:T(2,128)S(1)} all-to-all(f32[256,2,128]{2,1,0:T(2,128)S(1)} %bitcast.39), channel_id=1, replica_groups=mesh['ka'=32,'pa'=8] {'ka','pa'}, dimensions={0} | all-to-all | bytes 524288 | tf_op jit(solution)/shard_map/all_to_all | solution.py:191
  88.7 1.7 %shard_map.126 = (f32[256,256]{1,0:T(8,128)S(1)}, f32[512,128]{1,0:T(8,128)S(1)}) custom-call(f32[512,128]{1,0:T(8,128)S(1)} %bitcast.45, f32[8,3,32,256]{3,2,1,0:T(8,128)S(1)} %all-to-all-done.whole_ref, bf16[256,256]{1,0:T(8,128)(2,1)S(1)} %copy-done.12, bf16[256,256]{1,0:T(8,128)(2,1)S(1)} %copy-done.15), custom_call_target="tpu_custom_call" | custom-call | flops 402653184 | bytes 1572864 | tf_op jit(solution)/shard_map/pallas_call | solution.py:199
  90.4 21.2 %all_to_all.31 = f32[256,2,128]{2,1,0:T(2,128)S(1)} all-to-all(f32[256,2,128]{2,1,0:T(2,128)S(1)} %bitcast.46), channel_id=1, replica_groups=mesh['ka'=32,'pa'=8] {'ka','pa'}, dimensions={0} | all-to-all | bytes 524288 | tf_op jit(solution)/shard_map/all_to_all | solution.py:191
  111.5 0.7 shard_map.127
  112.2 0.0 copy-start.3
  112.2 21.3 %all_to_all.32 = f32[256,2,128]{2,1,0:T(2,128)S(1)} all-to-all(f32[256,2,128]{2,1,0:T(2,128)S(1)} %bitcast.38), channel_id=1, replica_groups=mesh['ka'=32,'pa'=8] {'ka','pa'}, dimensions={0} | all-to-all | bytes 524288 | tf_op jit(solution)/shard_map/all_to_all | solution.py:191
  133.5 0.9 shard_map.128
  134.4 22.3 %all_to_all.33 = f32[8,2,32,256]{3,2,1,0:T(8,128)S(1)} all-to-all(f32[8,2,32,256]{3,2,1,0:T(8,128)S(1)} %shard_map.128), channel_id=1, replica_groups=mesh['ka'=32,'pa'=8] {'pa'}, dimensions={0} | all-to-all | bytes 1048576 | tf_op jit(solution)/shard_map/all_to_all | solution.py:206
  156.7 0.9 fusion.2
  (21 shorter events, 0.0 us)
Async XLA Ops:
  0.6 50.9 %copy-start = (f32[256,8,32]{0,2,1:T(8,128)S(1)}, f32[256,8,32]{0,2,1:T(8,128)}, u32[]{:S(2)}) copy-start(f32[256,8,32]{0,2,1:T(8,128)} %param.16) | copy-start | bytes 786436
  0.6 14.9 %copy-start.1 = (f32[8,256,256]{2,1,0:T(8,128)S(1)}, f32[8,256,256]{2,1,0:T(8,128)}, u32[]{:S(2)}) copy-start(f32[8,256,256]{2,1,0:T(8,128)} %valence_ref.1) | copy-start | bytes 6291460
  0.7 1.1 copy-start.2
  1.8 0.9 copy-start.4
  2.7 0.9 copy-start.16
  3.7 0.9 copy-start.17
  5.6 34.1 %all-to-all-start = ((f32[8,3,32,256]{3,2,1,0:T(8,128)}), f32[8,3,32,256]{3,2,1,0:T(8,128)S(1)}, u32[]{:S(2)}, u32[]{:S(2)}) async-start(f32[8,3,32,256]{3,2,1,0:T(8,128)} %shard_map.122), calls=%async_computation | async-start | bytes 1572864 | tf_op jit(solution)/shard_map/all_to_all | solution.py:171
  15.6 51.2 %copy-start.6 = (bf16[256,256]{1,0:T(8,128)(2,1)S(1)}, bf16[256,256]{1,0:T(8,128)(2,1)}, u32[]{:S(2)}) copy-start(bf16[256,256]{1,0:T(8,128)(2,1)} %constant.22.clone.back_low) | copy-start | bytes 393220
  15.6 51.2 %copy-start.7 = (bf16[256,256]{1,0:T(8,128)(2,1)S(1)}, bf16[256,256]{1,0:T(8,128)(2,1)}, u32[]{:S(2)}) copy-start(bf16[256,256]{1,0:T(8,128)(2,1)} %constant.21.clone.back_high) | copy-start | bytes 393220
  15.6 51.1 %copy-start.8 = (bf16[256,256]{1,0:T(8,128)(2,1)S(1)}, bf16[256,256]{1,0:T(8,128)(2,1)}, u32[]{:S(2)}) copy-start(bf16[256,256]{1,0:T(8,128)(2,1)} %constant.20.clone.rows_low) | copy-start | bytes 393220
  15.8 0.7 copy-start.10
  16.5 0.7 copy-start.13
  17.1 49.6 %copy-start.9 = (bf16[256,256]{1,0:T(8,128)(2,1)S(1)}, bf16[256,256]{1,0:T(8,128)(2,1)}, u32[]{:S(2)}) copy-start(bf16[256,256]{1,0:T(8,128)(2,1)} %constant.19.clone.rows_high) | copy-start | bytes 393220
  39.7 0.9 copy-start.11
  40.6 0.9 copy-start.14
  41.5 47.2 %copy-start.12 = (bf16[256,256]{1,0:T(8,128)(2,1)S(1)}, bf16[256,256]{1,0:T(8,128)(2,1)}, u32[]{:S(2)}) copy-start(bf16[256,256]{1,0:T(8,128)(2,1)} %copy-done.10) | copy-start | bytes 393220
  41.5 47.2 %copy-start.15 = (bf16[256,256]{1,0:T(8,128)(2,1)S(1)}, bf16[256,256]{1,0:T(8,128)(2,1)}, u32[]{:S(2)}) copy-start(bf16[256,256]{1,0:T(8,128)(2,1)} %copy-done.13) | copy-start | bytes 393220
  43.1 23.7 %all-to-all-start.1 = ((f32[256,2,128]{2,1,0:T(2,128)}), f32[256,2,128]{2,1,0:T(2,128)S(1)}, u32[]{:S(2)}, u32[]{:S(2)}) async-start(f32[256,2,128]{2,1,0:T(2,128)} %bitcast.5), calls=%async_computation.1 | async-start | bytes 524288 | tf_op jit(solution)/shard_map/all_to_all | solution.py:191
  112.2 44.5 %copy-start.3 = (f32[8,256,32]{1,2,0:T(8,128)S(1)}, f32[8,256,32]{1,2,0:T(8,128)}, u32[]{:S(2)}) copy-start(f32[8,256,32]{1,2,0:T(8,128)} %param.12) | copy-start | bytes 786436
  112.2 44.5 %copy-start.5 = (f32[8,256,32]{1,2,0:T(8,128)S(1)}, f32[8,256,32]{1,2,0:T(8,128)}, u32[]{:S(2)}) copy-start(f32[8,256,32]{1,2,0:T(8,128)} %param.13) | copy-start | bytes 786436

commit v3 on v2

--- a/solution.py
+++ b/solution.py
@@ -83,16 +83,40 @@
     return jnp.concatenate(halves, axis=1)
 
 
-def pack_kernel(previous_ref, current_ref, energies_ref, conduction_ref, out_ref):
-    current = current_ref[...]
-    out_ref[:, 0] = current
-    out_ref[:, 1] = conduction_ref[...]
-    out_ref[:, 2] = 2.0 * energies_ref[...] * current - previous_ref[...]
-
-
-def valence_kernel(index_ref, valence_ref, high_ref, low_ref, turned_ref):
-    del index_ref
-    turned = valence_ref[0].T
+def pack_kernel(
+    index_ref, previous_ref, current_ref, energies_ref, conduction_ref, valence_ref, out_ref, mine_ref, given, packed, arrived, left
+):
+    count = packed.shape[0]
+    mine = pltpu.make_async_copy(valence_ref.at[index_ref[0]], mine_ref, left.at[count])
+
+    def arrivals(k):
+        pairs = (
+            (current_ref, packed.at[k, 0]),
+            (energies_ref, given.at[k, 0]),
+            (previous_ref, given.at[k, 1]),
+            (conduction_ref, packed.at[k, 1]),
+        )
+        return [pltpu.make_async_copy(ref.at[k], to, arrived.at[k, i]) for i, (ref, to) in enumerate(pairs)]
+
+    def departure(k):
+        return pltpu.make_async_copy(packed.at[k], out_ref.at[k], left.at[k])
+
+    for k in range(count):
+        for copy in arrivals(k):
+            copy.start()
+    mine.start()
+    for k in range(count):
+        for copy in arrivals(k):
+            copy.wait()
+        packed[k, 2] = 2.0 * given[k, 0] * packed[k, 0] - given[k, 1]
+        departure(k).start()
+    for k in range(count):
+        departure(k).wait()
+    mine.wait()
+
+
+def prepare_kernel(mine_ref, kernel_ref, pick_ref, high_ref, low_ref, weights_ref, turned_ref):
+    turned = mine_ref[...].T
     for half in range(2):
         columns = slice(half * LANES, (half + 1) * LANES)
         turned_ref[half] = turned[:, columns]
@@ -100,6 +124,14 @@
             high, low = split(turned_ref[half, pl.ds(row, 32, stride=8), :])
             high_ref[row * 32 : row * 32 + 32, columns] = high
             low_ref[row * 32 : row * 32 + 32, columns] = low
+    rest = kernel_ref[...]
+    total = rest.shape[0]
+    weights = jnp.zeros((total, total), F32)
+    for _ in range(3):
+        part = rest.astype(BF16)
+        rest = rest - part.astype(F32)
+        weights += lax.dot_general(pick_ref[...], part, NT, preferred_element_type=F32)
+    weights_ref[...] = weights * (1.0 / total)
 
 
 def square(ref, which):
@@ -165,26 +197,37 @@
     shaped = jax.ShapeDtypeStruct
     tables = [jnp.asarray(t) for t in (*split_table(rows), *split_table(rows.T.copy()))]
 
-    packed = call(pack_kernel, shaped((per_k, 3, slim, bands), F32), 3 * total**2, 7 * size)(
-        banded(previous), banded(current), banded(energies), banded(conduction)
+    far = pl.BlockSpec(memory_space=pl.ANY)
+    near = pl.BlockSpec(memory_space=pltpu.VMEM)
+    packed, mine = pl.pallas_call(
+        pack_kernel,
+        out_shape=[shaped((per_k, 3, slim, bands), F32), shaped((bands, total), F32)],
+        in_specs=[pl.BlockSpec(memory_space=pltpu.SMEM)] + [far] * 5,
+        out_specs=[far, near],
+        scratch_shapes=[
+            pltpu.VMEM((per_k, 2, slim, bands), F32),
+            pltpu.VMEM((per_k, 3, slim, bands), F32),
+            pltpu.SemaphoreType.DMA((per_k, 4)),
+            pltpu.SemaphoreType.DMA((per_k + 1,)),
+        ],
+        cost_estimate=pl.CostEstimate(flops=3 * total**2, bytes_accessed=8 * size, transcendentals=0),
+    )(
+        lax.axis_index("pa").reshape(1),
+        banded(previous),
+        banded(current),
+        banded(energies),
+        banded(conduction),
+        valence,
     )
     whole = lax.all_to_all(packed, "pa", split_axis=0, concat_axis=0, tiled=True)
 
-    high, low = call(
-        valence_kernel,
-        [shaped((total, bands), BF16)] * 2,
-        total**2,
-        2 * size,
-        grid_spec=pltpu.PrefetchScalarGridSpec(
-            num_scalar_prefetch=1,
-            grid=(1,),
-            in_specs=[pl.BlockSpec((1, bands, total), lambda i, index: (index[0], 0, 0))],
-            out_specs=[pl.BlockSpec((total, bands), lambda i, index: (0, 0))] * 2,
-            scratch_shapes=[pltpu.VMEM((2, total, LANES), F32)],
-        ),
-    )(lax.axis_index("pa").reshape(1), valence)
-    kernel_t = jnp.transpose(kernel, (1, 2, 0)).reshape(total, total)
-    weights = lax.dot_general(pick, kernel_t, NT, precision=lax.Precision.HIGHEST) / total
+    high, low, weights = call(
+        prepare_kernel,
+        [shaped((total, bands), BF16)] * 2 + [shaped((total, total), F32)],
+        3 * flops,
+        5 * size,
+        scratch_shapes=[pltpu.VMEM((2, total, LANES), F32)],
+    )(mine, jnp.transpose(kernel, (1, 2, 0)).reshape(total, total), jnp.asarray(pick.astype(BF16)))
 
     def exchange(block):
         block = block.reshape(total, 2, LANES)

time: 158 us -> 153 us (0.968)
  blocking collectives: 86 us -> 110 us
  waiting for transfers between devices: 36.4 us -> 22.8 us
  starting transfers between devices: 18.5 us -> 10.2 us
  local copies, waits for them, and re-layouts: 7.12 us -> 1 us
    all_to_all x3 -> x4, blocking collectives: 63.7 us -> 87.2 us  [exchange(): block = lax.all_to_all(block, both, split_axis=0, concat_axis=0, tiled=True)]
    all_to_all x1 -> x0, waiting for transfers between devices: 13.8 us -> none  [exchange(): block = lax.all_to_all(block, both, split_axis=0, concat_axis=0, tiled=True)]
    all_to_all x1 -> x0, starting transfers between devices: 8.5 us -> none  [exchange(): block = lax.all_to_all(block, both, split_axis=0, concat_axis=0, tiled=True)]
    unnamed x36 -> x18, local copies, waits for them, and re-layouts: 7.12 us -> 1 us
    pallas_call x2, Pallas kernels: 1.13 us -> 3.24 us  [the longest x1 2.93 us: on_device(): pl.pallas_call(pack_kernel, out_shape=[shaped((per_k, 3, slim, bands), F3...]
  transfers between devices with their start and end apart: 2 -> 1, of which waited for: 2 -> 1; matrix products, arithmetic and copies ran while one was open for 1% -> 0% of each run, Pallas kernels for 0% -> 0%
where the time goes in v3:
time: 153 us
  blocking collectives  110 us (72%)
  waiting for transfers between devices  22.8 us (15%)
  starting transfers between devices  10.2 us (7%)
  Pallas kernels  7.92 us (5%)
    all_to_all x4, blocking collectives, exchange(): block = lax.all_to_all(block, both, split_axis=0, concat_axis=0, tiled=True)  87.2 us
    all_to_all x1, waiting for transfers between devices, on_device(): lax.all_to_all(packed, 'pa', split_axis=0, concat_axis=0, tiled=True)  22.8 us
    all_to_all x1, blocking collectives, on_device(): home = lax.all_to_all(home, 'pa', split_axis=0, concat_axis=0, tiled=True)  22.3 us
    all_to_all x1, starting transfers between devices, on_device(): lax.all_to_all(packed, 'pa', split_axis=0, concat_axis=0, tiled=True)  10.2 us
  transfers between devices with their start and end apart: 1, of which 1 were waited for; matrix products, arithmetic and copies ran while one was open for 0% of the time, Pallas kernels for 0%

profile of v3, /device:TPU:32, one launch (start us, length us, event | category | flops | bytes accessed | tf_op | source)
XLA Modules:
  0.0 153.1 jit_solution(2478102326893939514)
XLA Ops:
  0.6 0.0 copy-start.4
  0.6 0.0 copy-start.6
  0.7 2.9 %shard_map.122 = (f32[8,3,32,256]{3,2,1,0:T(8,128)}, f32[256,256]{1,0:T(8,128)}) custom-call(s32[1]{0:T(128)} %bitcast.index_ref, f32[8,32,256]{2,1,0:T(8,128)} %bitcast.44, f32[8,32,256]{2,1,0:T(8,128)} %bitcast.42, f32[8,32,256]{2,1,0:T(8,128)} %bitcast.43, f32[8,32,256]{2,1,0:T(8,128)} %bitcast.45, f32[8,256,256]{2,1,0:T(8,128)} %valence_ref.1), custom_call_target="tpu_custom_call" | custom-call | flops 196608 | bytes 2097152 | tf_op jit(solution)/shard_map/pallas_call | solution.py:202
  3.6 0.0 copy-start
  3.6 0.0 copy-start.1
  3.6 0.0 copy-start.2
  3.6 0.0 copy-start.3
  3.6 10.2 %all-to-all-start = ((f32[8,3,32,256]{3,2,1,0:T(8,128)}), f32[8,3,32,256]{3,2,1,0:T(8,128)S(1)}, u32[]{:S(2)}, u32[]{:S(2)}) async-start(f32[8,3,32,256]{3,2,1,0:T(8,128)} %get-tuple-element.9), calls=%async_computation | async-start | bytes 1572864 | tf_op jit(solution)/shard_map/all_to_all | solution.py:222
  13.8 0.0 copy-done.4
  13.8 0.0 copy-done.6
  13.8 0.0 copy-start.5
  13.8 0.9 copy-done.5
  14.8 0.3 shard_map.123
  15.1 22.8 %all-to-all-done.whole_ref = f32[8,3,32,256]{3,2,1,0:T(8,128)S(1)} async-done(((f32[8,3,32,256]{3,2,1,0:T(8,128)}), f32[8,3,32,256]{3,2,1,0:T(8,128)S(1)}, u32[]{:S(2)}, u32[]{:S(2)}) %all-to-all-start) | async-done | bytes 786464 | tf_op jit(solution)/shard_map/all_to_all | solution.py:222
  37.9 0.8 shard_map.124
  38.8 23.6 %all_to_all.30 = f32[256,2,128]{2,1,0:T(2,128)S(1)} all-to-all(f32[256,2,128]{2,1,0:T(2,128)S(1)} %bitcast.37), channel_id=1, replica_groups=mesh['ka'=32,'pa'=8] {'ka','pa'}, dimensions={0} | all-to-all | bytes 524288 | tf_op jit(solution)/shard_map/all_to_all | solution.py:234
  62.4 0.0 copy-done
  62.4 0.0 copy-done.1
  62.4 0.0 copy-done.2
  62.4 0.0 copy-done.3
  62.4 0.7 shard_map.125
  63.0 21.2 %all_to_all.31 = f32[256,2,128]{2,1,0:T(2,128)S(1)} all-to-all(f32[256,2,128]{2,1,0:T(2,128)S(1)} %bitcast.36), channel_id=1, replica_groups=mesh['ka'=32,'pa'=8] {'ka','pa'}, dimensions={0} | all-to-all | bytes 524288 | tf_op jit(solution)/shard_map/all_to_all | solution.py:234
  84.2 1.7 %shard_map.126 = (f32[256,256]{1,0:T(8,128)S(1)}, f32[512,128]{1,0:T(8,128)S(1)}) custom-call(f32[512,128]{1,0:T(8,128)S(1)} %bitcast.40, f32[8,3,32,256]{3,2,1,0:T(8,128)S(1)} %all-to-all-done.whole_ref, bf16[256,256]{1,0:T(8,128)(2,1)S(1)} %get-tuple-element.11.high_ref, bf16[256,256]{1,0:T(8,128)(2,1)S(1)} %get-tuple-element.12.low_ref), custom_call_target="tpu_custom_call" | custom-call | flops 402653184 | bytes 1572864 | tf_op jit(solution)/shard_map/pallas_call | solution.py:242
  85.9 21.2 %all_to_all.32 = f32[256,2,128]{2,1,0:T(2,128)S(1)} all-to-all(f32[256,2,128]{2,1,0:T(2,128)S(1)} %bitcast.41), channel_id=1, replica_groups=mesh['ka'=32,'pa'=8] {'ka','pa'}, dimensions={0} | all-to-all | bytes 524288 | tf_op jit(solution)/shard_map/all_to_all | solution.py:234
  107.1 0.7 shard_map.127
  107.7 0.0 copy-start.7
  107.7 0.0 copy-start.8
  107.7 21.3 %all_to_all.33 = f32[256,2,128]{2,1,0:T(2,128)S(1)} all-to-all(f32[256,2,128]{2,1,0:T(2,128)S(1)} %bitcast.34), channel_id=1, replica_groups=mesh['ka'=32,'pa'=8] {'ka','pa'}, dimensions={0} | all-to-all | bytes 524288 | tf_op jit(solution)/shard_map/all_to_all | solution.py:234
  129.0 0.9 shard_map.128
  129.9 22.3 %all_to_all.34 = f32[8,2,32,256]{3,2,1,0:T(8,128)S(1)} all-to-all(f32[8,2,32,256]{3,2,1,0:T(8,128)S(1)} %shard_map.128), channel_id=1, replica_groups=mesh['ka'=32,'pa'=8] {'pa'}, dimensions={0} | all-to-all | bytes 1048576 | tf_op jit(solution)/shard_map/all_to_all | solution.py:249
  152.2 0.0 copy-done.8
  152.2 0.9 fusion.2
  (1 shorter events, 0.0 us)
Async XLA Ops:
  0.6 13.2 %copy-start.4 = (f32[256,8,32]{0,2,1:T(8,128)S(1)}, f32[256,8,32]{0,2,1:T(8,128)}, u32[]{:S(2)}) copy-start(f32[256,8,32]{0,2,1:T(8,128)} %param.16) | copy-start | bytes 786436
  0.6 13.2 %copy-start.6 = (bf16[256,256]{1,0:T(8,128)(2,1)S(1)}, bf16[256,256]{1,0:T(8,128)(2,1)}, u32[]{:S(2)}) copy-start(bf16[256,256]{1,0:T(8,128)(2,1)} %constant.20.clone.pick_ref) | copy-start | bytes 393220
  3.6 58.8 %copy-start = (bf16[256,256]{1,0:T(8,128)(2,1)S(1)}, bf16[256,256]{1,0:T(8,128)(2,1)}, u32[]{:S(2)}) copy-start(bf16[256,256]{1,0:T(8,128)(2,1)} %constant.19.clone.back_low) | copy-start | bytes 393220
  3.6 58.7 %copy-start.1 = (bf16[256,256]{1,0:T(8,128)(2,1)S(1)}, bf16[256,256]{1,0:T(8,128)(2,1)}, u32[]{:S(2)}) copy-start(bf16[256,256]{1,0:T(8,128)(2,1)} %constant.18.clone.back_high) | copy-start | bytes 393220
  3.6 58.7 %copy-start.2 = (bf16[256,256]{1,0:T(8,128)(2,1)S(1)}, bf16[256,256]{1,0:T(8,128)(2,1)}, u32[]{:S(2)}) copy-start(bf16[256,256]{1,0:T(8,128)(2,1)} %constant.17.clone.rows_low) | copy-start | bytes 393220
  3.6 58.7 %copy-start.3 = (bf16[256,256]{1,0:T(8,128)(2,1)S(1)}, bf16[256,256]{1,0:T(8,128)(2,1)}, u32[]{:S(2)}) copy-start(bf16[256,256]{1,0:T(8,128)(2,1)} %constant.16.clone.rows_high) | copy-start | bytes 393220
  3.6 34.3 %all-to-all-start = ((f32[8,3,32,256]{3,2,1,0:T(8,128)}), f32[8,3,32,256]{3,2,1,0:T(8,128)S(1)}, u32[]{:S(2)}, u32[]{:S(2)}) async-start(f32[8,3,32,256]{3,2,1,0:T(8,128)} %get-tuple-element.9), calls=%async_computation | async-start | bytes 1572864 | tf_op jit(solution)/shard_map/all_to_all | solution.py:222
  13.8 1.0 copy-start.5
  107.7 44.5 %copy-start.7 = (f32[8,256,32]{1,2,0:T(8,128)S(1)}, f32[8,256,32]{1,2,0:T(8,128)}, u32[]{:S(2)}) copy-start(f32[8,256,32]{1,2,0:T(8,128)} %param.12) | copy-start | bytes 786436
  107.7 44.5 %copy-start.8 = (f32[8,256,32]{1,2,0:T(8,128)S(1)}, f32[8,256,32]{1,2,0:T(8,128)}, u32[]{:S(2)}) copy-start(f32[8,256,32]{1,2,0:T(8,128)} %param.13) | copy-start | bytes 786436

commit v4 on v3

--- a/solution.py
+++ b/solution.py
@@ -47,8 +47,9 @@
 
 
 def dot3(a, b, dims=NN):
-    one = lambda p, q: lax.dot_general(p, q, dims, preferred_element_type=F32)
-    return one(a[0], b[0]) + (one(a[0], b[1]) + one(a[1], b[0]))
+    left = jnp.concatenate([a[0], a[0], a[1]], axis=1)
+    right = jnp.concatenate([b[0], b[1], b[0]], axis=dims[0][1][0])
+    return lax.dot_general(left, right, dims, preferred_element_type=F32)
 
 
 def swap_groups(blocks):
@@ -72,66 +73,80 @@
                 out_ref[pl.ds((half * 4 + p) * 2 + part, 32, stride=16), :] = block
 
 
-def load_messages(in_ref):
+def load_messages(in_ref, part):
     halves = []
     for half in range(2):
-        rows = []
-        for part in range(2):
-            blocks = [in_ref[pl.ds((half * 4 + p) * 2 + part, 32, stride=16), :] for p in range(4)]
-            rows.extend(swap_groups(blocks))
-        halves.append(jnp.concatenate(rows, axis=0))
+        blocks = [in_ref[pl.ds((half * 4 + p) * 2 + part, 32, stride=16), :] for p in range(4)]
+        halves.append(jnp.concatenate(swap_groups(blocks), axis=0))
     return jnp.concatenate(halves, axis=1)
 
 
 def pack_kernel(
-    index_ref, previous_ref, current_ref, energies_ref, conduction_ref, valence_ref, out_ref, mine_ref, given, packed, arrived, left
+    index_ref,
+    previous_ref,
+    current_ref,
+    energies_ref,
+    conduction_ref,
+    valence_ref,
+    kernel_ref,
+    pick_ref,
+    packed_ref,
+    high_ref,
+    low_ref,
+    weights_ref,
+    given,
+    mine,
+    momenta,
+    picked,
+    turned,
+    arrived,
+    fixed,
 ):
-    count = packed.shape[0]
-    mine = pltpu.make_async_copy(valence_ref.at[index_ref[0]], mine_ref, left.at[count])
+    count = packed_ref.shape[0]
+    copies = [
+        pltpu.make_async_copy(ref, to, fixed.at[i])
+        for i, (ref, to) in enumerate(
+            ((valence_ref.at[index_ref[0]], mine), (kernel_ref, momenta), (pick_ref, picked))
+        )
+    ]
 
     def arrivals(k):
         pairs = (
-            (current_ref, packed.at[k, 0]),
+            (current_ref, packed_ref.at[k, 0]),
             (energies_ref, given.at[k, 0]),
             (previous_ref, given.at[k, 1]),
-            (conduction_ref, packed.at[k, 1]),
+            (conduction_ref, packed_ref.at[k, 1]),
         )
         return [pltpu.make_async_copy(ref.at[k], to, arrived.at[k, i]) for i, (ref, to) in enumerate(pairs)]
 
-    def departure(k):
-        return pltpu.make_async_copy(packed.at[k], out_ref.at[k], left.at[k])
-
+    for copy in copies:
+        copy.start()
     for k in range(count):
         for copy in arrivals(k):
             copy.start()
-    mine.start()
-    for k in range(count):
-        for copy in arrivals(k):
-            copy.wait()
-        packed[k, 2] = 2.0 * given[k, 0] * packed[k, 0] - given[k, 1]
-        departure(k).start()
-    for k in range(count):
-        departure(k).wait()
-    mine.wait()
-
-
-def prepare_kernel(mine_ref, kernel_ref, pick_ref, high_ref, low_ref, weights_ref, turned_ref):
-    turned = mine_ref[...].T
+    copies[0].wait()
+    flipped = mine[...].T
     for half in range(2):
         columns = slice(half * LANES, (half + 1) * LANES)
-        turned_ref[half] = turned[:, columns]
+        turned[half] = flipped[:, columns]
         for row in range(8):
-            high, low = split(turned_ref[half, pl.ds(row, 32, stride=8), :])
+            high, low = split(turned[half, pl.ds(row, 32, stride=8), :])
             high_ref[row * 32 : row * 32 + 32, columns] = high
             low_ref[row * 32 : row * 32 + 32, columns] = low
-    rest = kernel_ref[...]
+    copies[1].wait()
+    copies[2].wait()
+    rest = momenta[...]
     total = rest.shape[0]
     weights = jnp.zeros((total, total), F32)
     for _ in range(3):
         part = rest.astype(BF16)
         rest = rest - part.astype(F32)
-        weights += lax.dot_general(pick_ref[...], part, NT, preferred_element_type=F32)
+        weights += lax.dot_general(picked[...], part, NT, preferred_element_type=F32)
     weights_ref[...] = weights * (1.0 / total)
+    for k in range(count):
+        for copy in arrivals(k):
+            copy.wait()
+        packed_ref[k, 2] = 2.0 * given[k, 0] * packed_ref[k, 0] - given[k, 1]
 
 
 def square(ref, which):
@@ -155,22 +170,30 @@
 
 
 def product_back(screened_ref, conduct, valence):
-    partial = dot3(split(load_messages(screened_ref)), conduct)
-    return dot3(split(partial.T), valence)
+    screened = jnp.concatenate([load_messages(screened_ref, part) for part in range(2)], axis=0)
+    return dot3(split(dot3(conduct, split(screened), NT)), valence)
+
+
+def product_back_by_halves(screened_ref, conduct, valence):
+    total = 0.0
+    for part in range(2):
+        mine = slice(part * LANES, (part + 1) * LANES)
+        partial = dot3(split(load_messages(screened_ref, part)), conduct)
+        total += dot3(split(partial.T), (valence[0][mine], valence[1][mine]))
+    return total
 
 
 def next_pairs_kernel(screened_ref, whole_ref, high_ref, low_ref, next_ref, out_ref):
     conduct = split(square(whole_ref, 1))
     valence = high_ref[...], low_ref[...]
-    following = square(whole_ref, 2) + 2.0 * product_back(screened_ref, conduct, valence)
+    following = square(whole_ref, 2) + 2.0 * product_back(screened_ref, split(square(whole_ref, 1).T), valence)
     next_ref[...] = following
     inner = dot3(conduct, split(following))
     store_messages(dot3(valence, split(inner), NT), out_ref)
 
 
 def last_kernel(screened_ref, whole_ref, high_ref, low_ref, next_ref, out_ref):
-    conduct = split(square(whole_ref, 1))
-    second = product_back(screened_ref, conduct, (high_ref[...], low_ref[...]))
+    second = product_back_by_halves(screened_ref, split(square(whole_ref, 1)), (high_ref[...], low_ref[...]))
     shape = out_ref.shape[0], out_ref.shape[2], out_ref.shape[3]
     out_ref[:, 0] = next_ref[...].reshape(shape)
     out_ref[:, 1] = second.reshape(shape)
@@ -197,37 +220,42 @@
     shaped = jax.ShapeDtypeStruct
     tables = [jnp.asarray(t) for t in (*split_table(rows), *split_table(rows.T.copy()))]
 
-    far = pl.BlockSpec(memory_space=pl.ANY)
+    far = pl.BlockSpec(memory_space=pltpu.HBM)
     near = pl.BlockSpec(memory_space=pltpu.VMEM)
-    packed, mine = pl.pallas_call(
+    packed, high, low, weights = pl.pallas_call(
         pack_kernel,
-        out_shape=[shaped((per_k, 3, slim, bands), F32), shaped((bands, total), F32)],
-        in_specs=[pl.BlockSpec(memory_space=pltpu.SMEM)] + [far] * 5,
-        out_specs=[far, near],
+        out_shape=[shaped((per_k, 3, slim, bands), F32)]
+        + [shaped((total, bands), BF16)] * 2
+        + [shaped((total, total), F32)],
+        in_specs=[pl.BlockSpec(memory_space=pltpu.SMEM)] + [far] * 7,
+        out_specs=[near] * 4,
         scratch_shapes=[
             pltpu.VMEM((per_k, 2, slim, bands), F32),
-            pltpu.VMEM((per_k, 3, slim, bands), F32),
+            pltpu.VMEM((bands, total), F32),
+            pltpu.VMEM((total, total), F32),
+            pltpu.VMEM((total, total), BF16),
+            pltpu.VMEM((2, total, LANES), F32),
             pltpu.SemaphoreType.DMA((per_k, 4)),
-            pltpu.SemaphoreType.DMA((per_k + 1,)),
+            pltpu.SemaphoreType.DMA((3,)),
         ],
-        cost_estimate=pl.CostEstimate(flops=3 * total**2, bytes_accessed=8 * size, transcendentals=0),
+        compiler_params=pltpu.CompilerParams(vmem_limit_bytes=VMEM_BYTES),
+        cost_estimate=pl.CostEstimate(flops=3 * flops, bytes_accessed=12 * size, transcendentals=0),
     )(
         lax.axis_index("pa").reshape(1),
-        banded(previous),
-        banded(current),
-        banded(energies),
-        banded(conduction),
-        valence,
+        *(
+            pltpu.with_memory_space_constraint(x, pltpu.HBM)
+            for x in (
+                banded(previous),
+                banded(current),
+                banded(energies),
+                banded(conduction),
+                valence,
+                jnp.transpose(kernel, (1, 2, 0)).reshape(total, total),
+                jnp.asarray(pick.astype(BF16)),
+            )
+        ),
     )
     whole = lax.all_to_all(packed, "pa", split_axis=0, concat_axis=0, tiled=True)
-
-    high, low, weights = call(
-        prepare_kernel,
-        [shaped((total, bands), BF16)] * 2 + [shaped((total, total), F32)],
-        3 * flops,
-        5 * size,
-        scratch_shapes=[pltpu.VMEM((2, total, LANES), F32)],
-    )(mine, jnp.transpose(kernel, (1, 2, 0)).reshape(total, total), jnp.asarray(pick.astype(BF16)))
 
     def exchange(block):
         block = block.reshape(total, 2, LANES)

time: 153 us -> 152 us (level)
  blocking collectives: 110 us -> 144 us
  waiting for transfers between devices: 22.8 us -> 0 us
  starting transfers between devices: 10.2 us -> 0 us
    all_to_all x0 -> x1, blocking collectives: none -> 35.1 us  [on_device(): lax.all_to_all(packed, 'pa', split_axis=0, concat_axis=0, tiled=True)]
    all_to_all x1 -> x0, waiting for transfers between devices: 22.8 us -> none  [on_device(): lax.all_to_all(packed, 'pa', split_axis=0, concat_axis=0, tiled=True)]
    all_to_all x1 -> x0, starting transfers between devices: 10.2 us -> none  [on_device(): lax.all_to_all(packed, 'pa', split_axis=0, concat_axis=0, tiled=True)]
  transfers between devices with their start and end apart: 1 -> 0, of which waited for: 1 -> 0; matrix products, arithmetic and copies ran while one was open for 0% -> 0% of each run, Pallas kernels for 0% -> 0%
where the time goes in v4:
time: 152 us
  blocking collectives  144 us (95%)
  Pallas kernels  6.78 us (4%)
    all_to_all x4, blocking collectives, exchange(): block = lax.all_to_all(block, both, split_axis=0, concat_axis=0, tiled=True)  86.2 us
    all_to_all x1, blocking collectives, on_device(): lax.all_to_all(packed, 'pa', split_axis=0, concat_axis=0, tiled=True)  35.1 us
    all_to_all x1, blocking collectives, on_device(): home = lax.all_to_all(home, 'pa', split_axis=0, concat_axis=0, tiled=True)  22.3 us

profile of v4, /device:TPU:32, one launch (start us, length us, event | category | flops | bytes accessed | tf_op | source)
XLA Modules:
  0.0 152.0 jit_solution(17771330358888639361)
XLA Ops:
  0.6 2.3 %shard_map.122 = (f32[8,3,32,256]{3,2,1,0:T(8,128)S(1)}, bf16[256,256]{1,0:T(8,128)(2,1)S(1)}, bf16[256,256]{1,0:T(8,128)(2,1)S(1)}, f32[256,256]{1,0:T(8,128)S(1)}) custom-call(s32[1]{0:T(128)} %bitcast.index_ref, f32[8,32,256]{2,1,0:T(8,128)} %bitcast.43, f32[8,32,256]{2,1,0:T(8,128)} %bitcast.41, f32[8,32,256]{2,1,0:T(8,128)} %bitcast.42, ...), custom_call_target="tpu_custom_call" | custom-call | flops 100663296 | bytes 3145728 | tf_op jit(solution)/shard_map/pallas_call | solution.py:225
  2.9 0.0 copy-start
  2.9 0.0 copy-start.1
  2.9 0.0 copy-start.2
  3.0 0.0 copy-start.3
  3.0 35.1 %all_to_all.30.whole_ref = f32[8,3,32,256]{3,2,1,0:T(8,128)S(1)} all-to-all(f32[8,3,32,256]{3,2,1,0:T(8,128)S(1)} %get-tuple-element.8), channel_id=1, replica_groups=mesh['ka'=32,'pa'=8] {'pa'}, dimensions={0} | all-to-all | bytes 1572864 | tf_op jit(solution)/shard_map/all_to_all | solution.py:258
  38.1 0.8 shard_map.123
  38.9 22.5 %all_to_all.31 = f32[256,2,128]{2,1,0:T(2,128)S(1)} all-to-all(f32[256,2,128]{2,1,0:T(2,128)S(1)} %bitcast.37), channel_id=1, replica_groups=mesh['ka'=32,'pa'=8] {'ka','pa'}, dimensions={0} | all-to-all | bytes 524288 | tf_op jit(solution)/shard_map/all_to_all | solution.py:262
  61.5 0.0 copy-done
  61.5 0.0 copy-done.1
  61.5 0.0 copy-done.2
  61.5 0.0 copy-done.3
  61.5 0.7 shard_map.124
  62.2 21.2 %all_to_all.32 = f32[256,2,128]{2,1,0:T(2,128)S(1)} all-to-all(f32[256,2,128]{2,1,0:T(2,128)S(1)} %bitcast.36), channel_id=1, replica_groups=mesh['ka'=32,'pa'=8] {'ka','pa'}, dimensions={0} | all-to-all | bytes 524288 | tf_op jit(solution)/shard_map/all_to_all | solution.py:262
  83.3 1.6 %shard_map.125 = (f32[256,256]{1,0:T(8,128)S(1)}, f32[512,128]{1,0:T(8,128)S(1)}) custom-call(f32[512,128]{1,0:T(8,128)S(1)} %bitcast.39, f32[8,3,32,256]{3,2,1,0:T(8,128)S(1)} %all_to_all.30.whole_ref, bf16[256,256]{1,0:T(8,128)(2,1)S(1)} %get-tuple-element.9.high_ref, bf16[256,256]{1,0:T(8,128)(2,1)S(1)} %get-tuple-element.10.low_ref), custom_call_target="tpu_custom_call" | custom-call | flops 402653184 | bytes 1572864 | tf_op jit(solution)/shard_map/pallas_call | solution.py:270
  85.0 21.2 %all_to_all.33 = f32[256,2,128]{2,1,0:T(2,128)S(1)} all-to-all(f32[256,2,128]{2,1,0:T(2,128)S(1)} %bitcast.40), channel_id=1, replica_groups=mesh['ka'=32,'pa'=8] {'ka','pa'}, dimensions={0} | all-to-all | bytes 524288 | tf_op jit(solution)/shard_map/all_to_all | solution.py:262
  106.1 0.7 shard_map.126
  106.8 0.0 copy-start.4
  106.8 0.0 copy-start.5
  106.8 21.3 %all_to_all.34 = f32[256,2,128]{2,1,0:T(2,128)S(1)} all-to-all(f32[256,2,128]{2,1,0:T(2,128)S(1)} %bitcast.34), channel_id=1, replica_groups=mesh['ka'=32,'pa'=8] {'ka','pa'}, dimensions={0} | all-to-all | bytes 524288 | tf_op jit(solution)/shard_map/all_to_all | solution.py:262
  128.1 0.7 shard_map.127
  128.8 22.3 %all_to_all.35 = f32[8,2,32,256]{3,2,1,0:T(8,128)S(1)} all-to-all(f32[8,2,32,256]{3,2,1,0:T(8,128)S(1)} %shard_map.127), channel_id=1, replica_groups=mesh['ka'=32,'pa'=8] {'pa'}, dimensions={0} | all-to-all | bytes 1048576 | tf_op jit(solution)/shard_map/all_to_all | solution.py:277
  151.2 0.0 copy-done.4
  151.2 0.0 copy-done.5
  151.2 0.9 fusion.2
Async XLA Ops:
  2.9 58.5 %copy-start = (bf16[256,256]{1,0:T(8,128)(2,1)S(1)}, bf16[256,256]{1,0:T(8,128)(2,1)}, u32[]{:S(2)}) copy-start(bf16[256,256]{1,0:T(8,128)(2,1)} %constant.19.clone.back_low) | copy-start | bytes 393220
  2.9 58.5 %copy-start.1 = (bf16[256,256]{1,0:T(8,128)(2,1)S(1)}, bf16[256,256]{1,0:T(8,128)(2,1)}, u32[]{:S(2)}) copy-start(bf16[256,256]{1,0:T(8,128)(2,1)} %constant.18.clone.back_high) | copy-start | bytes 393220
  2.9 58.5 %copy-start.2 = (bf16[256,256]{1,0:T(8,128)(2,1)S(1)}, bf16[256,256]{1,0:T(8,128)(2,1)}, u32[]{:S(2)}) copy-start(bf16[256,256]{1,0:T(8,128)(2,1)} %constant.17.clone.rows_low) | copy-start | bytes 393220
  3.0 58.5 %copy-start.3 = (bf16[256,256]{1,0:T(8,128)(2,1)S(1)}, bf16[256,256]{1,0:T(8,128)(2,1)}, u32[]{:S(2)}) copy-start(bf16[256,256]{1,0:T(8,128)(2,1)} %constant.16.clone.rows_high) | copy-start | bytes 393220
  106.8 44.4 %copy-start.4 = (f32[8,256,32]{1,2,0:T(8,128)S(1)}, f32[8,256,32]{1,2,0:T(8,128)}, u32[]{:S(2)}) copy-start(f32[8,256,32]{1,2,0:T(8,128)} %param.12) | copy-start | bytes 786436
  106.8 44.4 %copy-start.5 = (f32[8,256,32]{1,2,0:T(8,128)S(1)}, f32[8,256,32]{1,2,0:T(8,128)}, u32[]{:S(2)}) copy-start(f32[8,256,32]{1,2,0:T(8,128)} %param.13) | copy-start | bytes 786436

commit v5 on v4

--- a/solution.py
+++ b/solution.py
@@ -102,28 +102,25 @@
     arrived,
     fixed,
 ):
-    count = packed_ref.shape[0]
+    fields = [
+        pltpu.make_async_copy(ref, to, arrived.at[i])
+        for i, (ref, to) in enumerate(
+            (
+                (current_ref, packed_ref.at[:, 0]),
+                (energies_ref, given.at[0]),
+                (previous_ref, given.at[1]),
+                (conduction_ref, packed_ref.at[:, 1]),
+            )
+        )
+    ]
     copies = [
         pltpu.make_async_copy(ref, to, fixed.at[i])
         for i, (ref, to) in enumerate(
             ((valence_ref.at[index_ref[0]], mine), (kernel_ref, momenta), (pick_ref, picked))
         )
     ]
-
-    def arrivals(k):
-        pairs = (
-            (current_ref, packed_ref.at[k, 0]),
-            (energies_ref, given.at[k, 0]),
-            (previous_ref, given.at[k, 1]),
-            (conduction_ref, packed_ref.at[k, 1]),
-        )
-        return [pltpu.make_async_copy(ref.at[k], to, arrived.at[k, i]) for i, (ref, to) in enumerate(pairs)]
-
-    for copy in copies:
+    for copy in copies + fields:
         copy.start()
-    for k in range(count):
-        for copy in arrivals(k):
-            copy.start()
     copies[0].wait()
     flipped = mine[...].T
     for half in range(2):
@@ -143,10 +140,9 @@
         rest = rest - part.astype(F32)
         weights += lax.dot_general(picked[...], part, NT, preferred_element_type=F32)
     weights_ref[...] = weights * (1.0 / total)
-    for k in range(count):
-        for copy in arrivals(k):
-            copy.wait()
-        packed_ref[k, 2] = 2.0 * given[k, 0] * packed_ref[k, 0] - given[k, 1]
+    for copy in fields:
+        copy.wait()
+    packed_ref[:, 2] = 2.0 * given[0] * packed_ref[:, 0] - given[1]
 
 
 def square(ref, which):
@@ -162,9 +158,12 @@
 
 def screen_kernel(owned_ref, rows_high, rows_low, back_high, back_low, weights_ref, out_ref):
     total = weights_ref.shape[0]
-    owned = jnp.concatenate([owned_ref[pl.ds(part, total, stride=2), :] for part in range(2)], axis=1)
-    modes = dot3((rows_high[...], rows_low[...]), split(owned)) * weights_ref[...]
-    screened = dot3((back_high[...], back_low[...]), split(modes))
+    owned = split(jnp.concatenate([owned_ref[pl.ds(part, total, stride=2), :] for part in range(2)], axis=1))
+    screened = 0.0
+    for part in range(2):
+        mine = slice(part * LANES, (part + 1) * LANES)
+        modes = dot3((rows_high[mine], rows_low[mine]), owned) * weights_ref[mine]
+        screened += dot3((back_high[:, mine], back_low[:, mine]), split(modes))
     for part in range(2):
         out_ref[pl.ds(part, total, stride=2), :] = screened[:, part * LANES : (part + 1) * LANES]
 
@@ -230,12 +229,12 @@
         in_specs=[pl.BlockSpec(memory_space=pltpu.SMEM)] + [far] * 7,
         out_specs=[near] * 4,
         scratch_shapes=[
-            pltpu.VMEM((per_k, 2, slim, bands), F32),
+            pltpu.VMEM((2, per_k, slim, bands), F32),
             pltpu.VMEM((bands, total), F32),
             pltpu.VMEM((total, total), F32),
             pltpu.VMEM((total, total), BF16),
             pltpu.VMEM((2, total, LANES), F32),
-            pltpu.SemaphoreType.DMA((per_k, 4)),
+            pltpu.SemaphoreType.DMA((4,)),
             pltpu.SemaphoreType.DMA((3,)),
         ],
         compiler_params=pltpu.CompilerParams(vmem_limit_bytes=VMEM_BYTES),

time: 152 us -> 152 us (level)
  no operation moved by 1% of the time
where the time goes in v5:
time: 152 us; the launch traced here: 151 us
  blocking collectives  144 us (95%)
  Pallas kernels  6.01 us (4%)
    all_to_all x4, blocking collectives, exchange(): block = lax.all_to_all(block, both, split_axis=0, concat_axis=0, tiled=True)  86.2 us
    all_to_all x1, blocking collectives, on_device(): lax.all_to_all(packed, 'pa', split_axis=0, concat_axis=0, tiled=True)  35.1 us
    all_to_all x1, blocking collectives, on_device(): home = lax.all_to_all(home, 'pa', split_axis=0, concat_axis=0, tiled=True)  22.3 us

profile of v5, /device:TPU:32, one launch (start us, length us, event | category | flops | bytes accessed | tf_op | source)
XLA Modules:
  0.0 151.3 jit_solution(14591589968645326469)
XLA Ops:
  0.6 1.7 %shard_map.122 = (f32[8,3,32,256]{3,2,1,0:T(8,128)S(1)}, bf16[256,256]{1,0:T(8,128)(2,1)S(1)}, bf16[256,256]{1,0:T(8,128)(2,1)S(1)}, f32[256,256]{1,0:T(8,128)S(1)}) custom-call(s32[1]{0:T(128)} %bitcast.index_ref, f32[8,32,256]{2,1,0:T(8,128)} %bitcast.43, f32[8,32,256]{2,1,0:T(8,128)} %bitcast.41, f32[8,32,256]{2,1,0:T(8,128)} %bitcast.42, ...), custom_call_target="tpu_custom_call" | custom-call | flops 100663296 | bytes 3145728 | tf_op jit(solution)/shard_map/pallas_call | solution.py:224
  2.4 0.0 copy-start
  2.4 0.0 copy-start.1
  2.4 0.0 copy-start.2
  2.4 0.0 copy-start.3
  2.4 35.1 %all_to_all.30.whole_ref = f32[8,3,32,256]{3,2,1,0:T(8,128)S(1)} all-to-all(f32[8,3,32,256]{3,2,1,0:T(8,128)S(1)} %get-tuple-element.8), channel_id=1, replica_groups=mesh['ka'=32,'pa'=8] {'pa'}, dimensions={0} | all-to-all | bytes 1572864 | tf_op jit(solution)/shard_map/all_to_all | solution.py:257
  37.6 0.8 shard_map.123
  38.4 22.5 %all_to_all.31 = f32[256,2,128]{2,1,0:T(2,128)S(1)} all-to-all(f32[256,2,128]{2,1,0:T(2,128)S(1)} %bitcast.37), channel_id=1, replica_groups=mesh['ka'=32,'pa'=8] {'ka','pa'}, dimensions={0} | all-to-all | bytes 524288 | tf_op jit(solution)/shard_map/all_to_all | solution.py:261
  60.9 0.0 copy-done
  60.9 0.0 copy-done.1
  60.9 0.0 copy-done.2
  60.9 0.0 copy-done.3
  60.9 0.6 shard_map.124
  61.5 21.2 %all_to_all.32 = f32[256,2,128]{2,1,0:T(2,128)S(1)} all-to-all(f32[256,2,128]{2,1,0:T(2,128)S(1)} %bitcast.36), channel_id=1, replica_groups=mesh['ka'=32,'pa'=8] {'ka','pa'}, dimensions={0} | all-to-all | bytes 524288 | tf_op jit(solution)/shard_map/all_to_all | solution.py:261
  82.7 1.6 %shard_map.125 = (f32[256,256]{1,0:T(8,128)S(1)}, f32[512,128]{1,0:T(8,128)S(1)}) custom-call(f32[512,128]{1,0:T(8,128)S(1)} %bitcast.39, f32[8,3,32,256]{3,2,1,0:T(8,128)S(1)} %all_to_all.30.whole_ref, bf16[256,256]{1,0:T(8,128)(2,1)S(1)} %get-tuple-element.9.high_ref, bf16[256,256]{1,0:T(8,128)(2,1)S(1)} %get-tuple-element.10.low_ref), custom_call_target="tpu_custom_call" | custom-call | flops 402653184 | bytes 1572864 | tf_op jit(solution)/shard_map/pallas_call | solution.py:269
  84.3 21.2 %all_to_all.33 = f32[256,2,128]{2,1,0:T(2,128)S(1)} all-to-all(f32[256,2,128]{2,1,0:T(2,128)S(1)} %bitcast.40), channel_id=1, replica_groups=mesh['ka'=32,'pa'=8] {'ka','pa'}, dimensions={0} | all-to-all | bytes 524288 | tf_op jit(solution)/shard_map/all_to_all | solution.py:261
  105.5 0.6 shard_map.126
  106.0 0.0 copy-start.4
  106.0 0.0 copy-start.5
  106.1 21.3 %all_to_all.34 = f32[256,2,128]{2,1,0:T(2,128)S(1)} all-to-all(f32[256,2,128]{2,1,0:T(2,128)S(1)} %bitcast.34), channel_id=1, replica_groups=mesh['ka'=32,'pa'=8] {'ka','pa'}, dimensions={0} | all-to-all | bytes 524288 | tf_op jit(solution)/shard_map/all_to_all | solution.py:261
  127.4 0.7 shard_map.127
  128.1 22.3 %all_to_all.35 = f32[8,2,32,256]{3,2,1,0:T(8,128)S(1)} all-to-all(f32[8,2,32,256]{3,2,1,0:T(8,128)S(1)} %shard_map.127), channel_id=1, replica_groups=mesh['ka'=32,'pa'=8] {'pa'}, dimensions={0} | all-to-all | bytes 1048576 | tf_op jit(solution)/shard_map/all_to_all | solution.py:276
  150.4 0.0 copy-done.4
  150.4 0.0 copy-done.5
  150.4 0.9 fusion.2
Async XLA Ops:
  2.4 58.5 %copy-start = (bf16[256,256]{1,0:T(8,128)(2,1)S(1)}, bf16[256,256]{1,0:T(8,128)(2,1)}, u32[]{:S(2)}) copy-start(bf16[256,256]{1,0:T(8,128)(2,1)} %constant.19.clone.back_low) | copy-start | bytes 393220
  2.4 58.5 %copy-start.1 = (bf16[256,256]{1,0:T(8,128)(2,1)S(1)}, bf16[256,256]{1,0:T(8,128)(2,1)}, u32[]{:S(2)}) copy-start(bf16[256,256]{1,0:T(8,128)(2,1)} %constant.18.clone.back_high) | copy-start | bytes 393220
  2.4 58.5 %copy-start.2 = (bf16[256,256]{1,0:T(8,128)(2,1)S(1)}, bf16[256,256]{1,0:T(8,128)(2,1)}, u32[]{:S(2)}) copy-start(bf16[256,256]{1,0:T(8,128)(2,1)} %constant.17.clone.rows_low) | copy-start | bytes 393220
  2.4 58.5 %copy-start.3 = (bf16[256,256]{1,0:T(8,128)(2,1)S(1)}, bf16[256,256]{1,0:T(8,128)(2,1)}, u32[]{:S(2)}) copy-start(bf16[256,256]{1,0:T(8,128)(2,1)} %constant.16.clone.rows_high) | copy-start | bytes 393220
  106.0 44.4 %copy-start.4 = (f32[8,256,32]{1,2,0:T(8,128)S(1)}, f32[8,256,32]{1,2,0:T(8,128)}, u32[]{:S(2)}) copy-start(f32[8,256,32]{1,2,0:T(8,128)} %param.12) | copy-start | bytes 786436
  106.0 44.4 %copy-start.5 = (f32[8,256,32]{1,2,0:T(8,128)S(1)}, f32[8,256,32]{1,2,0:T(8,128)}, u32[]{:S(2)}) copy-start(f32[8,256,32]{1,2,0:T(8,128)} %param.13) | copy-start | bytes 786436

commit v6 on v5

--- a/solution.py
+++ b/solution.py
@@ -52,32 +52,32 @@
     return lax.dot_general(left, right, dims, preferred_element_type=F32)
 
 
-def swap_groups(blocks):
-    lane = lax.broadcasted_iota(jnp.int32, blocks[0].shape, 1)
-    low = lane < 64
-    a, b, c, d = blocks
-    turn = lambda x, by: pltpu.roll(x, by, 1)
-    a, c = jnp.where(low, a, turn(c, 64)), jnp.where(low, turn(a, 64), c)
-    b, d = jnp.where(low, b, turn(d, 64)), jnp.where(low, turn(b, 64), d)
-    even = (lane // 32) % 2 == 0
-    a, b = jnp.where(even, a, turn(b, 32)), jnp.where(even, turn(a, 96), b)
-    c, d = jnp.where(even, c, turn(d, 32)), jnp.where(even, turn(c, 96), d)
-    return a, b, c, d
+def choose(blocks, which):
+    group = lax.broadcasted_iota(jnp.int32, blocks[0].shape, 1) // 32
+    chosen = [blocks[(g - which) % 4] for g in range(4)]
+    low = jnp.where(group == 0, chosen[0], chosen[1])
+    high = jnp.where(group == 2, chosen[2], chosen[3])
+    return jnp.where(group < 2, low, high)
 
 
 def store_messages(pairs, out_ref):
     for half in range(2):
         for part in range(2):
-            blocks = [pairs[(4 * part + i) * 32 : (4 * part + i) * 32 + 32, half * LANES : (half + 1) * LANES] for i in range(4)]
-            for p, block in enumerate(swap_groups(blocks)):
-                out_ref[pl.ds((half * 4 + p) * 2 + part, 32, stride=16), :] = block
+            blocks = []
+            for i in range(4):
+                start = (4 * part + i) * 32
+                block = pairs[start : start + 32, half * LANES : (half + 1) * LANES]
+                blocks.append(pltpu.roll(block, 32 * i, 1) if i else block)
+            for p in range(4):
+                out_ref[pl.ds((half * 4 + p) * 2 + part, 32, stride=16), :] = choose(blocks, p)
 
 
 def load_messages(in_ref, part):
     halves = []
     for half in range(2):
         blocks = [in_ref[pl.ds((half * 4 + p) * 2 + part, 32, stride=16), :] for p in range(4)]
-        halves.append(jnp.concatenate(swap_groups(blocks), axis=0))
+        rows = [choose(blocks, i) for i in range(4)]
+        halves.append(jnp.concatenate([pltpu.roll(x, LANES - 32 * i, 1) if i else x for i, x in enumerate(rows)], axis=0))
     return jnp.concatenate(halves, axis=1)
 
 
@@ -132,7 +132,9 @@
             low_ref[row * 32 : row * 32 + 32, columns] = low
     copies[1].wait()
     copies[2].wait()
-    rest = momenta[...]
+    turn = index_ref[0] % 4
+    starts = [pl.multiple_of((4 * part + (g + 4 - turn) % 4) * 32, 32) for part in range(2) for g in range(4)]
+    rest = jnp.concatenate([momenta[pl.ds(start, 32), :] for start in starts], axis=0)
     total = rest.shape[0]
     weights = jnp.zeros((total, total), F32)
     for _ in range(3):
@@ -150,49 +152,55 @@
     return block.reshape(block.shape[0] * block.shape[1], block.shape[2])
 
 
-def first_pairs_kernel(whole_ref, high_ref, low_ref, out_ref):
+def first_pairs_kernel(whole_ref, high_ref, low_ref, out_ref, turned_high_ref, turned_low_ref):
     conduct = split(square(whole_ref, 1))
-    inner = dot3(conduct, split(square(whole_ref, 0)))
-    store_messages(dot3((high_ref[...], low_ref[...]), split(inner), NT), out_ref)
+    field = split(square(whole_ref, 0))
+    inner = [split(dot3((conduct[0][rows], conduct[1][rows]), field)) for rows in (slice(0, LANES), slice(LANES, None))]
+    inner = [jnp.concatenate([inner[0][i], inner[1][i]], axis=0) for i in range(2)]
+    turned_high_ref[...], turned_low_ref[...] = split(square(whole_ref, 1).T)
+    store_messages(dot3((high_ref[...], low_ref[...]), inner, NT), out_ref)
 
 
 def screen_kernel(owned_ref, rows_high, rows_low, back_high, back_low, weights_ref, out_ref):
     total = weights_ref.shape[0]
     owned = split(jnp.concatenate([owned_ref[pl.ds(part, total, stride=2), :] for part in range(2)], axis=1))
-    screened = 0.0
+    modes = []
     for part in range(2):
         mine = slice(part * LANES, (part + 1) * LANES)
-        modes = dot3((rows_high[mine], rows_low[mine]), owned) * weights_ref[mine]
-        screened += dot3((back_high[:, mine], back_low[:, mine]), split(modes))
-    for part in range(2):
-        out_ref[pl.ds(part, total, stride=2), :] = screened[:, part * LANES : (part + 1) * LANES]
-
-
-def product_back(screened_ref, conduct, valence):
+        modes.append(split(dot3((rows_high[mine], rows_low[mine]), owned) * weights_ref[mine]))
+    modes = [jnp.concatenate([modes[0][i], modes[1][i]], axis=0) for i in range(2)]
+    for piece in range(2):
+        mine = slice(piece * LANES, (piece + 1) * LANES)
+        screened = dot3((back_high[mine], back_low[mine]), modes)
+        for part in range(2):
+            lines = pl.ds(2 * piece * LANES + part, LANES, stride=2)
+            out_ref[lines, :] = screened[:, part * LANES : (part + 1) * LANES]
+
+
+def product_back(screened_ref, turned, valence):
     screened = jnp.concatenate([load_messages(screened_ref, part) for part in range(2)], axis=0)
-    return dot3(split(dot3(conduct, split(screened), NT)), valence)
-
-
-def product_back_by_halves(screened_ref, conduct, valence):
-    total = 0.0
+    return dot3(split(dot3(turned, split(screened), NT)), valence)
+
+
+def next_pairs_kernel(screened_ref, whole_ref, high_ref, low_ref, turned_high_ref, turned_low_ref, next_ref, out_ref):
+    conduct = split(square(whole_ref, 1))
+    turned = turned_high_ref[...], turned_low_ref[...]
+    valence = high_ref[...], low_ref[...]
+    following = square(whole_ref, 2) + 2.0 * product_back(screened_ref, turned, valence)
+    next_ref[...] = following
+    field = split(following)
+    inner = [split(dot3((conduct[0][rows], conduct[1][rows]), field)) for rows in (slice(0, LANES), slice(LANES, None))]
+    inner = [jnp.concatenate([inner[0][i], inner[1][i]], axis=0) for i in range(2)]
+    store_messages(dot3(valence, inner, NT), out_ref)
+
+
+def last_kernel(screened_ref, whole_ref, high_ref, low_ref, next_ref, out_ref):
+    conduct = split(square(whole_ref, 1))
+    second = 0.0
     for part in range(2):
         mine = slice(part * LANES, (part + 1) * LANES)
         partial = dot3(split(load_messages(screened_ref, part)), conduct)
-        total += dot3(split(partial.T), (valence[0][mine], valence[1][mine]))
-    return total
-
-
-def next_pairs_kernel(screened_ref, whole_ref, high_ref, low_ref, next_ref, out_ref):
-    conduct = split(square(whole_ref, 1))
-    valence = high_ref[...], low_ref[...]
-    following = square(whole_ref, 2) + 2.0 * product_back(screened_ref, split(square(whole_ref, 1).T), valence)
-    next_ref[...] = following
-    inner = dot3(conduct, split(following))
-    store_messages(dot3(valence, split(inner), NT), out_ref)
-
-
-def last_kernel(screened_ref, whole_ref, high_ref, low_ref, next_ref, out_ref):
-    second = product_back_by_halves(screened_ref, split(square(whole_ref, 1)), (high_ref[...], low_ref[...]))
+        second += dot3(split(partial.T), (high_ref[mine, :], low_ref[mine, :]))
     shape = out_ref.shape[0], out_ref.shape[2], out_ref.shape[3]
     out_ref[:, 0] = next_ref[...].reshape(shape)
     out_ref[:, 1] = second.reshape(shape)
@@ -264,10 +272,11 @@
     message = shaped((2 * total, LANES), F32)
     screen = call(screen_kernel, message, 6 * flops, 5 * size)
 
-    pairs = call(first_pairs_kernel, message, 6 * flops, 4 * size)(whole, high, low)
+    part = shaped((total, total), BF16)
+    pairs, *turned = call(first_pairs_kernel, [message, part, part], 6 * flops, 5 * size)(whole, high, low)
     back = exchange(screen(exchange(pairs), *tables, weights))
     following, pairs = call(next_pairs_kernel, [shaped((total, bands), F32), message], 12 * flops, 6 * size)(
-        back, whole, high, low
+        back, whole, high, low, *turned
     )
     back = exchange(screen(exchange(pairs), *tables, weights))
     home = call(last_kernel, shaped((per_k, 2, slim, bands), F32), 6 * flops, 6 * size)(

time: 152 us -> 151 us (level)
  no operation moved by 1% of the time
where the time goes in v6:
time: 151 us
  blocking collectives  144 us (95%)
  Pallas kernels  5.52 us (4%)
    all_to_all x4, blocking collectives, exchange(): block = lax.all_to_all(block, both, split_axis=0, concat_axis=0, tiled=True)  86.2 us
    all_to_all x1, blocking collectives, on_device(): lax.all_to_all(packed, 'pa', split_axis=0, concat_axis=0, tiled=True)  35.1 us
    all_to_all x1, blocking collectives, on_device(): home = lax.all_to_all(home, 'pa', split_axis=0, concat_axis=0, tiled=True)  22.3 us

profile of v6, /device:TPU:32, one launch (start us, length us, event | category | flops | bytes accessed | tf_op | source)
XLA Modules:
  0.0 150.8 jit_solution(6797438245405663120)
XLA Ops:
  0.6 1.7 %shard_map.122 = (f32[8,3,32,256]{3,2,1,0:T(8,128)S(1)}, bf16[256,256]{1,0:T(8,128)(2,1)S(1)}, bf16[256,256]{1,0:T(8,128)(2,1)S(1)}, f32[256,256]{1,0:T(8,128)S(1)}) custom-call(s32[1]{0:T(128)} %bitcast.index_ref, f32[8,32,256]{2,1,0:T(8,128)} %bitcast.43, f32[8,32,256]{2,1,0:T(8,128)} %bitcast.41, f32[8,32,256]{2,1,0:T(8,128)} %bitcast.42, ...), custom_call_target="tpu_custom_call" | custom-call | flops 100663296 | bytes 3145728 | tf_op jit(solution)/shard_map/pallas_call | solution.py:232
  2.4 0.0 copy-start
  2.4 0.0 copy-start.1
  2.4 0.0 copy-start.2
  2.4 0.0 copy-start.3
  2.4 35.1 %all_to_all.30.whole_ref = f32[8,3,32,256]{3,2,1,0:T(8,128)S(1)} all-to-all(f32[8,3,32,256]{3,2,1,0:T(8,128)S(1)} %get-tuple-element.11), channel_id=1, replica_groups=mesh['ka'=32,'pa'=8] {'pa'}, dimensions={0} | all-to-all | bytes 1572864 | tf_op jit(solution)/shard_map/all_to_all | solution.py:265
  37.6 0.7 shard_map.123
  38.2 22.5 %all_to_all.31 = f32[256,2,128]{2,1,0:T(2,128)S(1)} all-to-all(f32[256,2,128]{2,1,0:T(2,128)S(1)} %bitcast.40), channel_id=1, replica_groups=mesh['ka'=32,'pa'=8] {'ka','pa'}, dimensions={0} | all-to-all | bytes 524288 | tf_op jit(solution)/shard_map/all_to_all | solution.py:269
  60.8 0.0 copy-done
  60.8 0.0 copy-done.1
  60.8 0.0 copy-done.2
  60.8 0.0 copy-done.3
  60.8 0.5 shard_map.124
  61.3 21.2 %all_to_all.32 = f32[256,2,128]{2,1,0:T(2,128)S(1)} all-to-all(f32[256,2,128]{2,1,0:T(2,128)S(1)} %bitcast.36), channel_id=1, replica_groups=mesh['ka'=32,'pa'=8] {'ka','pa'}, dimensions={0} | all-to-all | bytes 524288 | tf_op jit(solution)/shard_map/all_to_all | solution.py:269
  82.5 1.4 shard_map.125
  83.9 21.2 %all_to_all.33 = f32[256,2,128]{2,1,0:T(2,128)S(1)} all-to-all(f32[256,2,128]{2,1,0:T(2,128)S(1)} %bitcast.39), channel_id=1, replica_groups=mesh['ka'=32,'pa'=8] {'ka','pa'}, dimensions={0} | all-to-all | bytes 524288 | tf_op jit(solution)/shard_map/all_to_all | solution.py:269
  105.0 0.5 shard_map.126
  105.6 0.0 copy-start.4
  105.6 0.0 copy-start.5
  105.6 21.3 %all_to_all.34 = f32[256,2,128]{2,1,0:T(2,128)S(1)} all-to-all(f32[256,2,128]{2,1,0:T(2,128)S(1)} %bitcast.34), channel_id=1, replica_groups=mesh['ka'=32,'pa'=8] {'ka','pa'}, dimensions={0} | all-to-all | bytes 524288 | tf_op jit(solution)/shard_map/all_to_all | solution.py:269
  126.9 0.7 shard_map.127
  127.6 22.3 %all_to_all.35 = f32[8,2,32,256]{3,2,1,0:T(8,128)S(1)} all-to-all(f32[8,2,32,256]{3,2,1,0:T(8,128)S(1)} %shard_map.127), channel_id=1, replica_groups=mesh['ka'=32,'pa'=8] {'pa'}, dimensions={0} | all-to-all | bytes 1048576 | tf_op jit(solution)/shard_map/all_to_all | solution.py:285
  149.9 0.0 copy-done.4
  149.9 0.0 copy-done.5
  149.9 0.9 fusion.2
Async XLA Ops:
  2.4 58.4 %copy-start = (bf16[256,256]{1,0:T(8,128)(2,1)S(1)}, bf16[256,256]{1,0:T(8,128)(2,1)}, u32[]{:S(2)}) copy-start(bf16[256,256]{1,0:T(8,128)(2,1)} %constant.19.clone.back_low) | copy-start | bytes 393220
  2.4 58.4 %copy-start.1 = (bf16[256,256]{1,0:T(8,128)(2,1)S(1)}, bf16[256,256]{1,0:T(8,128)(2,1)}, u32[]{:S(2)}) copy-start(bf16[256,256]{1,0:T(8,128)(2,1)} %constant.18.clone.back_high) | copy-start | bytes 393220
  2.4 58.4 %copy-start.2 = (bf16[256,256]{1,0:T(8,128)(2,1)S(1)}, bf16[256,256]{1,0:T(8,128)(2,1)}, u32[]{:S(2)}) copy-start(bf16[256,256]{1,0:T(8,128)(2,1)} %constant.17.clone.rows_low) | copy-start | bytes 393220
  2.4 58.4 %copy-start.3 = (bf16[256,256]{1,0:T(8,128)(2,1)S(1)}, bf16[256,256]{1,0:T(8,128)(2,1)}, u32[]{:S(2)}) copy-start(bf16[256,256]{1,0:T(8,128)(2,1)} %constant.16.clone.rows_high) | copy-start | bytes 393220
  105.6 44.3 %copy-start.4 = (f32[8,256,32]{1,2,0:T(8,128)S(1)}, f32[8,256,32]{1,2,0:T(8,128)}, u32[]{:S(2)}) copy-start(f32[8,256,32]{1,2,0:T(8,128)} %param.12) | copy-start | bytes 786436
  105.6 44.3 %copy-start.5 = (f32[8,256,32]{1,2,0:T(8,128)S(1)}, f32[8,256,32]{1,2,0:T(8,128)}, u32[]{:S(2)}) copy-start(f32[8,256,32]{1,2,0:T(8,128)} %param.13) | copy-start | bytes 786436

commit v7 on v6

--- a/solution.py
+++ b/solution.py
@@ -22,18 +22,20 @@
     points = np.arange(total)
     coarse, finer = points // KY, points % KY
     mirror = (-coarse % wide) * KY + (-finer % KY)
-    alone = [q for q in range(total) if mirror[q] == q]
-    paired = [q for q in range(total) if q < mirror[q]]
     turns = (coarse[:, None] * coarse[None, :] % wide) / wide
     turns = turns + (finer[:, None] * finer[None, :] % KY) / KY
     angles = 2.0 * math.pi * turns
-    cosine, sine = np.cos(angles), np.sin(angles)
-    rows = np.concatenate([cosine[alone], cosine[paired], sine[paired]])
-    pick = np.zeros((total, total))
-    for i, q in enumerate(alone + paired + paired):
-        pick[i, q] = 1.0
-        pick[i, mirror[q]] = 1.0
-    return rows.astype(np.float32), pick.astype(np.float32)
+    rows = np.where((points <= mirror)[:, None], np.cos(angles), np.sin(angles))
+    return rows.astype(np.float32)
+
+
+def pair_sums(total):
+    row = lax.broadcasted_iota(jnp.int32, (total, total), 0)
+    column = lax.broadcasted_iota(jnp.int32, (total, total), 1)
+    wide = total // KY
+    bits = KY.bit_length() - 1
+    mirror = (((wide - (row >> bits)) & (wide - 1)) << bits) + ((KY - (row & (KY - 1))) & (KY - 1))
+    return jnp.where((column == row) | (column == mirror), 1.0, 0.0).astype(BF16)
 
 
 def split_table(table):
@@ -89,7 +91,6 @@
     conduction_ref,
     valence_ref,
     kernel_ref,
-    pick_ref,
     packed_ref,
     high_ref,
     low_ref,
@@ -97,7 +98,6 @@
     given,
     mine,
     momenta,
-    picked,
     turned,
     arrived,
     fixed,
@@ -116,7 +116,7 @@
     copies = [
         pltpu.make_async_copy(ref, to, fixed.at[i])
         for i, (ref, to) in enumerate(
-            ((valence_ref.at[index_ref[0]], mine), (kernel_ref, momenta), (pick_ref, picked))
+            ((valence_ref.at[index_ref[0]], mine), (kernel_ref, momenta))
         )
     ]
     for copy in copies + fields:
@@ -131,16 +131,14 @@
             high_ref[row * 32 : row * 32 + 32, columns] = high
             low_ref[row * 32 : row * 32 + 32, columns] = low
     copies[1].wait()
-    copies[2].wait()
     turn = index_ref[0] % 4
     starts = [pl.multiple_of((4 * part + (g + 4 - turn) % 4) * 32, 32) for part in range(2) for g in range(4)]
     rest = jnp.concatenate([momenta[pl.ds(start, 32), :] for start in starts], axis=0)
     total = rest.shape[0]
     weights = jnp.zeros((total, total), F32)
-    for _ in range(3):
-        part = rest.astype(BF16)
-        rest = rest - part.astype(F32)
-        weights += lax.dot_general(picked[...], part, NT, preferred_element_type=F32)
+    picked = pair_sums(total)
+    for part in split(rest):
+        weights += lax.dot_general(picked, part, NT, preferred_element_type=F32)
     weights_ref[...] = weights * (1.0 / total)
     for copy in fields:
         copy.wait()
@@ -218,7 +216,7 @@
 
 def on_device(previous, current, energies, valence, conduction, kernel):
     total = kernel.shape[0]
-    rows, pick = real_transform(total)
+    rows = real_transform(total)
     both = ("ka", "pa")
     banded = lambda x: jnp.swapaxes(x, 1, 2)
     per_k, bands, slim = current.shape
@@ -234,16 +232,15 @@
         out_shape=[shaped((per_k, 3, slim, bands), F32)]
         + [shaped((total, bands), BF16)] * 2
         + [shaped((total, total), F32)],
-        in_specs=[pl.BlockSpec(memory_space=pltpu.SMEM)] + [far] * 7,
+        in_specs=[pl.BlockSpec(memory_space=pltpu.SMEM)] + [far] * 6,
         out_specs=[near] * 4,
         scratch_shapes=[
             pltpu.VMEM((2, per_k, slim, bands), F32),
             pltpu.VMEM((bands, total), F32),
             pltpu.VMEM((total, total), F32),
-            pltpu.VMEM((total, total), BF16),
             pltpu.VMEM((2, total, LANES), F32),
             pltpu.SemaphoreType.DMA((4,)),
-            pltpu.SemaphoreType.DMA((3,)),
+            pltpu.SemaphoreType.DMA((2,)),
         ],
         compiler_params=pltpu.CompilerParams(vmem_limit_bytes=VMEM_BYTES),
         cost_estimate=pl.CostEstimate(flops=3 * flops, bytes_accessed=12 * size, transcendentals=0),
@@ -258,7 +255,6 @@
                 banded(conduction),
                 valence,
                 jnp.transpose(kernel, (1, 2, 0)).reshape(total, total),
-                jnp.asarray(pick.astype(BF16)),
             )
         ),
     )

time: 151 us -> 151 us (level)
  no operation moved by 1% of the time
where the time goes in v7:
time: 151 us
  blocking collectives  144 us (95%)
  Pallas kernels  5.48 us (4%)
    all_to_all x4, blocking collectives, exchange(): block = lax.all_to_all(block, both, split_axis=0, concat_axis=0, tiled=True)  86.2 us
    all_to_all x1, blocking collectives, on_device(): lax.all_to_all(packed, 'pa', split_axis=0, concat_axis=0, tiled=True)  35.1 us
    all_to_all x1, blocking collectives, on_device(): home = lax.all_to_all(home, 'pa', split_axis=0, concat_axis=0, tiled=True)  22.3 us

profile of v7, /device:TPU:32, one launch (start us, length us, event | category | flops | bytes accessed | tf_op | source)
XLA Modules:
  0.0 150.7 jit_solution(11084388234050527251)
XLA Ops:
  0.6 1.7 %shard_map.113 = (f32[8,3,32,256]{3,2,1,0:T(8,128)S(1)}, bf16[256,256]{1,0:T(8,128)(2,1)S(1)}, bf16[256,256]{1,0:T(8,128)(2,1)S(1)}, f32[256,256]{1,0:T(8,128)S(1)}) custom-call(s32[1]{0:T(128)} %bitcast.index_ref, f32[8,32,256]{2,1,0:T(8,128)} %bitcast.43, f32[8,32,256]{2,1,0:T(8,128)} %bitcast.41, f32[8,32,256]{2,1,0:T(8,128)} %bitcast.42, ...), custom_call_target="tpu_custom_call" | custom-call | flops 100663296 | bytes 3145728 | tf_op jit(solution)/shard_map/pallas_call | solution.py:230
  2.3 0.0 copy-start
  2.4 0.0 copy-start.1
  2.4 0.0 copy-start.2
  2.4 0.0 copy-start.3
  2.4 35.1 %all_to_all.30.whole_ref = f32[8,3,32,256]{3,2,1,0:T(8,128)S(1)} all-to-all(f32[8,3,32,256]{3,2,1,0:T(8,128)S(1)} %get-tuple-element.11), channel_id=1, replica_groups=mesh['ka'=32,'pa'=8] {'pa'}, dimensions={0} | all-to-all | bytes 1572864 | tf_op jit(solution)/shard_map/all_to_all | solution.py:261
  37.5 0.7 shard_map.114
  38.2 22.5 %all_to_all.31 = f32[256,2,128]{2,1,0:T(2,128)S(1)} all-to-all(f32[256,2,128]{2,1,0:T(2,128)S(1)} %bitcast.40), channel_id=1, replica_groups=mesh['ka'=32,'pa'=8] {'ka','pa'}, dimensions={0} | all-to-all | bytes 524288 | tf_op jit(solution)/shard_map/all_to_all | solution.py:265
  60.7 0.0 copy-done
  60.7 0.0 copy-done.1
  60.7 0.0 copy-done.2
  60.7 0.0 copy-done.3
  60.7 0.5 shard_map.115
  61.3 21.2 %all_to_all.32 = f32[256,2,128]{2,1,0:T(2,128)S(1)} all-to-all(f32[256,2,128]{2,1,0:T(2,128)S(1)} %bitcast.36), channel_id=1, replica_groups=mesh['ka'=32,'pa'=8] {'ka','pa'}, dimensions={0} | all-to-all | bytes 524288 | tf_op jit(solution)/shard_map/all_to_all | solution.py:265
  82.4 1.4 shard_map.116
  83.8 21.2 %all_to_all.33 = f32[256,2,128]{2,1,0:T(2,128)S(1)} all-to-all(f32[256,2,128]{2,1,0:T(2,128)S(1)} %bitcast.39), channel_id=1, replica_groups=mesh['ka'=32,'pa'=8] {'ka','pa'}, dimensions={0} | all-to-all | bytes 524288 | tf_op jit(solution)/shard_map/all_to_all | solution.py:265
  105.0 0.5 shard_map.117
  105.5 0.0 copy-start.4
  105.5 0.0 copy-start.5
  105.6 21.3 %all_to_all.34 = f32[256,2,128]{2,1,0:T(2,128)S(1)} all-to-all(f32[256,2,128]{2,1,0:T(2,128)S(1)} %bitcast.34), channel_id=1, replica_groups=mesh['ka'=32,'pa'=8] {'ka','pa'}, dimensions={0} | all-to-all | bytes 524288 | tf_op jit(solution)/shard_map/all_to_all | solution.py:265
  126.8 0.7 shard_map.118
  127.5 22.3 %all_to_all.35 = f32[8,2,32,256]{3,2,1,0:T(8,128)S(1)} all-to-all(f32[8,2,32,256]{3,2,1,0:T(8,128)S(1)} %shard_map.118), channel_id=1, replica_groups=mesh['ka'=32,'pa'=8] {'pa'}, dimensions={0} | all-to-all | bytes 1048576 | tf_op jit(solution)/shard_map/all_to_all | solution.py:281
  149.9 0.0 copy-done.4
  149.9 0.0 copy-done.5
  149.9 0.9 fusion.2
Async XLA Ops:
  2.3 58.4 %copy-start = (bf16[256,256]{1,0:T(8,128)(2,1)S(1)}, bf16[256,256]{1,0:T(8,128)(2,1)}, u32[]{:S(2)}) copy-start(bf16[256,256]{1,0:T(8,128)(2,1)} %constant.17.clone.back_low) | copy-start | bytes 393220
  2.4 58.4 %copy-start.1 = (bf16[256,256]{1,0:T(8,128)(2,1)S(1)}, bf16[256,256]{1,0:T(8,128)(2,1)}, u32[]{:S(2)}) copy-start(bf16[256,256]{1,0:T(8,128)(2,1)} %constant.16.clone.back_high) | copy-start | bytes 393220
  2.4 58.4 %copy-start.2 = (bf16[256,256]{1,0:T(8,128)(2,1)S(1)}, bf16[256,256]{1,0:T(8,128)(2,1)}, u32[]{:S(2)}) copy-start(bf16[256,256]{1,0:T(8,128)(2,1)} %constant.15.clone.rows_low) | copy-start | bytes 393220
  2.4 58.4 %copy-start.3 = (bf16[256,256]{1,0:T(8,128)(2,1)S(1)}, bf16[256,256]{1,0:T(8,128)(2,1)}, u32[]{:S(2)}) copy-start(bf16[256,256]{1,0:T(8,128)(2,1)} %constant.14.clone.rows_high) | copy-start | bytes 393220
  105.5 44.3 %copy-start.4 = (f32[8,256,32]{1,2,0:T(8,128)S(1)}, f32[8,256,32]{1,2,0:T(8,128)}, u32[]{:S(2)}) copy-start(f32[8,256,32]{1,2,0:T(8,128)} %param.11) | copy-start | bytes 786436
  105.5 44.3 %copy-start.5 = (f32[8,256,32]{1,2,0:T(8,128)S(1)}, f32[8,256,32]{1,2,0:T(8,128)}, u32[]{:S(2)}) copy-start(f32[8,256,32]{1,2,0:T(8,128)} %param.12) | copy-start | bytes 786436

commit v8 on v7

--- a/solution.py
+++ b/solution.py
@@ -150,8 +150,9 @@
     return block.reshape(block.shape[0] * block.shape[1], block.shape[2])
 
 
-def first_pairs_kernel(whole_ref, high_ref, low_ref, out_ref, turned_high_ref, turned_low_ref):
+def first_pairs_kernel(whole_ref, high_ref, low_ref, out_ref, turned_high_ref, turned_low_ref, conduct_high_ref, conduct_low_ref):
     conduct = split(square(whole_ref, 1))
+    conduct_high_ref[...], conduct_low_ref[...] = conduct
     field = split(square(whole_ref, 0))
     inner = [split(dot3((conduct[0][rows], conduct[1][rows]), field)) for rows in (slice(0, LANES), slice(LANES, None))]
     inner = [jnp.concatenate([inner[0][i], inner[1][i]], axis=0) for i in range(2)]
@@ -180,8 +181,8 @@
     return dot3(split(dot3(turned, split(screened), NT)), valence)
 
 
-def next_pairs_kernel(screened_ref, whole_ref, high_ref, low_ref, turned_high_ref, turned_low_ref, next_ref, out_ref):
-    conduct = split(square(whole_ref, 1))
+def next_pairs_kernel(screened_ref, whole_ref, high_ref, low_ref, turned_high_ref, turned_low_ref, conduct_high_ref, conduct_low_ref, next_ref, out_ref):
+    conduct = conduct_high_ref[...], conduct_low_ref[...]
     turned = turned_high_ref[...], turned_low_ref[...]
     valence = high_ref[...], low_ref[...]
     following = square(whole_ref, 2) + 2.0 * product_back(screened_ref, turned, valence)
@@ -192,8 +193,8 @@
     store_messages(dot3(valence, inner, NT), out_ref)
 
 
-def last_kernel(screened_ref, whole_ref, high_ref, low_ref, next_ref, out_ref):
-    conduct = split(square(whole_ref, 1))
+def last_kernel(screened_ref, high_ref, low_ref, conduct_high_ref, conduct_low_ref, next_ref, out_ref):
+    conduct = conduct_high_ref[...], conduct_low_ref[...]
     second = 0.0
     for part in range(2):
         mine = slice(part * LANES, (part + 1) * LANES)
@@ -269,14 +270,14 @@
     screen = call(screen_kernel, message, 6 * flops, 5 * size)
 
     part = shaped((total, total), BF16)
-    pairs, *turned = call(first_pairs_kernel, [message, part, part], 6 * flops, 5 * size)(whole, high, low)
+    pairs, *parts = call(first_pairs_kernel, [message] + [part] * 4, 6 * flops, 5 * size)(whole, high, low)
     back = exchange(screen(exchange(pairs), *tables, weights))
     following, pairs = call(next_pairs_kernel, [shaped((total, bands), F32), message], 12 * flops, 6 * size)(
-        back, whole, high, low, *turned
+        back, whole, high, low, *parts
     )
     back = exchange(screen(exchange(pairs), *tables, weights))
     home = call(last_kernel, shaped((per_k, 2, slim, bands), F32), 6 * flops, 6 * size)(
-        back, whole, high, low, following
+        back, high, low, *parts[2:], following
     )
     home = lax.all_to_all(home, "pa", split_axis=0, concat_axis=0, tiled=True)
     next_one = banded(home[:, 0])

time: 151 us -> 151 us (level)
  no operation moved by 1% of the time
where the time goes in v8:
time: 151 us
  blocking collectives  143 us (95%)
  Pallas kernels  5.48 us (4%)
    all_to_all x4, blocking collectives, exchange(): block = lax.all_to_all(block, both, split_axis=0, concat_axis=0, tiled=True)  86 us
    all_to_all x1, blocking collectives, on_device(): lax.all_to_all(packed, 'pa', split_axis=0, concat_axis=0, tiled=True)  35.1 us
    all_to_all x1, blocking collectives, on_device(): home = lax.all_to_all(home, 'pa', split_axis=0, concat_axis=0, tiled=True)  22.3 us

profile of v8, /device:TPU:32, one launch (start us, length us, event | category | flops | bytes accessed | tf_op | source)
XLA Modules:
  0.0 150.6 jit_solution(16001608517993896861)
XLA Ops:
  0.6 1.7 %shard_map.113 = (f32[8,3,32,256]{3,2,1,0:T(8,128)S(1)}, bf16[256,256]{1,0:T(8,128)(2,1)S(1)}, bf16[256,256]{1,0:T(8,128)(2,1)S(1)}, f32[256,256]{1,0:T(8,128)S(1)}) custom-call(s32[1]{0:T(128)} %bitcast.index_ref, f32[8,32,256]{2,1,0:T(8,128)} %bitcast.43, f32[8,32,256]{2,1,0:T(8,128)} %bitcast.41, f32[8,32,256]{2,1,0:T(8,128)} %bitcast.42, ...), custom_call_target="tpu_custom_call" | custom-call | flops 100663296 | bytes 3145728 | tf_op jit(solution)/shard_map/pallas_call | solution.py:231
  2.3 0.0 copy-start
  2.4 0.0 copy-start.1
  2.4 0.0 copy-start.2
  2.4 0.0 copy-start.3
  2.4 35.1 %all_to_all.30.whole_ref = f32[8,3,32,256]{3,2,1,0:T(8,128)S(1)} all-to-all(f32[8,3,32,256]{3,2,1,0:T(8,128)S(1)} %get-tuple-element.13), channel_id=1, replica_groups=mesh['ka'=32,'pa'=8] {'pa'}, dimensions={0} | all-to-all | bytes 1572864 | tf_op jit(solution)/shard_map/all_to_all | solution.py:262
  37.5 0.7 shard_map.114
  38.2 22.5 %all_to_all.31 = f32[256,2,128]{2,1,0:T(2,128)S(1)} all-to-all(f32[256,2,128]{2,1,0:T(2,128)S(1)} %bitcast.40), channel_id=1, replica_groups=mesh['ka'=32,'pa'=8] {'ka','pa'}, dimensions={0} | all-to-all | bytes 524288 | tf_op jit(solution)/shard_map/all_to_all | solution.py:266
  60.7 0.0 copy-done
  60.7 0.0 copy-done.1
  60.7 0.0 copy-done.2
  60.7 0.0 copy-done.3
  60.8 0.5 shard_map.115
  61.3 21.2 %all_to_all.32 = f32[256,2,128]{2,1,0:T(2,128)S(1)} all-to-all(f32[256,2,128]{2,1,0:T(2,128)S(1)} %bitcast.37), channel_id=1, replica_groups=mesh['ka'=32,'pa'=8] {'ka','pa'}, dimensions={0} | all-to-all | bytes 524288 | tf_op jit(solution)/shard_map/all_to_all | solution.py:266
  82.5 1.4 shard_map.116
  83.8 21.2 %all_to_all.33 = f32[256,2,128]{2,1,0:T(2,128)S(1)} all-to-all(f32[256,2,128]{2,1,0:T(2,128)S(1)} %bitcast.39), channel_id=1, replica_groups=mesh['ka'=32,'pa'=8] {'ka','pa'}, dimensions={0} | all-to-all | bytes 524288 | tf_op jit(solution)/shard_map/all_to_all | solution.py:266
  105.0 0.0 copy-start.4
  105.0 0.0 copy-start.5
  105.0 0.5 shard_map.117
  105.5 21.2 %all_to_all.34 = f32[256,2,128]{2,1,0:T(2,128)S(1)} all-to-all(f32[256,2,128]{2,1,0:T(2,128)S(1)} %bitcast.35), channel_id=1, replica_groups=mesh['ka'=32,'pa'=8] {'ka','pa'}, dimensions={0} | all-to-all | bytes 524288 | tf_op jit(solution)/shard_map/all_to_all | solution.py:266
  126.7 0.7 shard_map.118
  127.4 22.3 %all_to_all.35 = f32[8,2,32,256]{3,2,1,0:T(8,128)S(1)} all-to-all(f32[8,2,32,256]{3,2,1,0:T(8,128)S(1)} %shard_map.118), channel_id=1, replica_groups=mesh['ka'=32,'pa'=8] {'pa'}, dimensions={0} | all-to-all | bytes 1048576 | tf_op jit(solution)/shard_map/all_to_all | solution.py:282
  149.7 0.0 copy-done.4
  149.7 0.0 copy-done.5
  149.7 0.9 fusion.2
Async XLA Ops:
  2.3 58.4 %copy-start = (bf16[256,256]{1,0:T(8,128)(2,1)S(1)}, bf16[256,256]{1,0:T(8,128)(2,1)}, u32[]{:S(2)}) copy-start(bf16[256,256]{1,0:T(8,128)(2,1)} %constant.17.clone.back_low) | copy-start | bytes 393220
  2.4 58.4 %copy-start.1 = (bf16[256,256]{1,0:T(8,128)(2,1)S(1)}, bf16[256,256]{1,0:T(8,128)(2,1)}, u32[]{:S(2)}) copy-start(bf16[256,256]{1,0:T(8,128)(2,1)} %constant.16.clone.back_high) | copy-start | bytes 393220
  2.4 58.4 %copy-start.2 = (bf16[256,256]{1,0:T(8,128)(2,1)S(1)}, bf16[256,256]{1,0:T(8,128)(2,1)}, u32[]{:S(2)}) copy-start(bf16[256,256]{1,0:T(8,128)(2,1)} %constant.15.clone.rows_low) | copy-start | bytes 393220
  2.4 58.4 %copy-start.3 = (bf16[256,256]{1,0:T(8,128)(2,1)S(1)}, bf16[256,256]{1,0:T(8,128)(2,1)}, u32[]{:S(2)}) copy-start(bf16[256,256]{1,0:T(8,128)(2,1)} %constant.14.clone.rows_high) | copy-start | bytes 393220
  105.0 44.7 %copy-start.4 = (f32[8,256,32]{1,2,0:T(8,128)S(1)}, f32[8,256,32]{1,2,0:T(8,128)}, u32[]{:S(2)}) copy-start(f32[8,256,32]{1,2,0:T(8,128)} %param.11) | copy-start | bytes 786436
  105.0 44.7 %copy-start.5 = (f32[8,256,32]{1,2,0:T(8,128)S(1)}, f32[8,256,32]{1,2,0:T(8,128)}, u32[]{:S(2)}) copy-start(f32[8,256,32]{1,2,0:T(8,128)} %param.12) | copy-start | bytes 786436

commit v9 on v8

--- a/solution.py
+++ b/solution.py
@@ -186,7 +186,7 @@
     turned = turned_high_ref[...], turned_low_ref[...]
     valence = high_ref[...], low_ref[...]
     following = square(whole_ref, 2) + 2.0 * product_back(screened_ref, turned, valence)
-    next_ref[...] = following
+    next_ref[:, 0] = following.reshape(next_ref.shape[0], next_ref.shape[2], next_ref.shape[3])
     field = split(following)
     inner = [split(dot3((conduct[0][rows], conduct[1][rows]), field)) for rows in (slice(0, LANES), slice(LANES, None))]
     inner = [jnp.concatenate([inner[0][i], inner[1][i]], axis=0) for i in range(2)]
@@ -194,6 +194,7 @@
 
 
 def last_kernel(screened_ref, high_ref, low_ref, conduct_high_ref, conduct_low_ref, next_ref, out_ref):
+    del next_ref
     conduct = conduct_high_ref[...], conduct_low_ref[...]
     second = 0.0
     for part in range(2):
@@ -201,7 +202,6 @@
         partial = dot3(split(load_messages(screened_ref, part)), conduct)
         second += dot3(split(partial.T), (high_ref[mine, :], low_ref[mine, :]))
     shape = out_ref.shape[0], out_ref.shape[2], out_ref.shape[3]
-    out_ref[:, 0] = next_ref[...].reshape(shape)
     out_ref[:, 1] = second.reshape(shape)
 
 
@@ -272,11 +272,11 @@
     part = shaped((total, total), BF16)
     pairs, *parts = call(first_pairs_kernel, [message] + [part] * 4, 6 * flops, 5 * size)(whole, high, low)
     back = exchange(screen(exchange(pairs), *tables, weights))
-    following, pairs = call(next_pairs_kernel, [shaped((total, bands), F32), message], 12 * flops, 6 * size)(
+    following, pairs = call(next_pairs_kernel, [shaped((per_k, 2, slim, bands), F32), message], 12 * flops, 6 * size)(
         back, whole, high, low, *parts
     )
     back = exchange(screen(exchange(pairs), *tables, weights))
-    home = call(last_kernel, shaped((per_k, 2, slim, bands), F32), 6 * flops, 6 * size)(
+    home = call(last_kernel, shaped((per_k, 2, slim, bands), F32), 6 * flops, 6 * size, input_output_aliases={5: 0})(
         back, high, low, *parts[2:], following
     )
     home = lax.all_to_all(home, "pa", split_axis=0, concat_axis=0, tiled=True)

time: 151 us -> 151 us (level)
  no operation moved by 1% of the time
where the time goes in v9:
time: 151 us
  blocking collectives  143 us (95%)
  Pallas kernels  5.48 us (4%)
    all_to_all x4, blocking collectives, exchange(): block = lax.all_to_all(block, both, split_axis=0, concat_axis=0, tiled=True)  86 us
    all_to_all x1, blocking collectives, on_device(): lax.all_to_all(packed, 'pa', split_axis=0, concat_axis=0, tiled=True)  35.1 us
    all_to_all x1, blocking collectives, on_device(): home = lax.all_to_all(home, 'pa', split_axis=0, concat_axis=0, tiled=True)  22.3 us

profile of v9, /device:TPU:32, one launch (start us, length us, event | category | flops | bytes accessed | tf_op | source)
XLA Modules:
  0.0 150.6 jit_solution(7226364899794560330)
XLA Ops:
  0.6 1.7 %shard_map.113 = (f32[8,3,32,256]{3,2,1,0:T(8,128)S(1)}, bf16[256,256]{1,0:T(8,128)(2,1)S(1)}, bf16[256,256]{1,0:T(8,128)(2,1)S(1)}, f32[256,256]{1,0:T(8,128)S(1)}) custom-call(s32[1]{0:T(128)} %bitcast.index_ref, f32[8,32,256]{2,1,0:T(8,128)} %bitcast.43, f32[8,32,256]{2,1,0:T(8,128)} %bitcast.41, f32[8,32,256]{2,1,0:T(8,128)} %bitcast.42, ...), custom_call_target="tpu_custom_call" | custom-call | flops 100663296 | bytes 3145728 | tf_op jit(solution)/shard_map/pallas_call | solution.py:231
  2.3 0.0 copy-start
  2.4 0.0 copy-start.1
  2.4 0.0 copy-start.2
  2.4 0.0 copy-start.3
  2.4 35.1 %all_to_all.30.whole_ref = f32[8,3,32,256]{3,2,1,0:T(8,128)S(1)} all-to-all(f32[8,3,32,256]{3,2,1,0:T(8,128)S(1)} %get-tuple-element.13), channel_id=1, replica_groups=mesh['ka'=32,'pa'=8] {'pa'}, dimensions={0} | all-to-all | bytes 1572864 | tf_op jit(solution)/shard_map/all_to_all | solution.py:262
  37.5 0.7 shard_map.114
  38.2 22.5 %all_to_all.31 = f32[256,2,128]{2,1,0:T(2,128)S(1)} all-to-all(f32[256,2,128]{2,1,0:T(2,128)S(1)} %bitcast.40), channel_id=1, replica_groups=mesh['ka'=32,'pa'=8] {'ka','pa'}, dimensions={0} | all-to-all | bytes 524288 | tf_op jit(solution)/shard_map/all_to_all | solution.py:266
  60.7 0.0 copy-done
  60.7 0.0 copy-done.1
  60.7 0.0 copy-done.2
  60.7 0.0 copy-done.3
  60.8 0.5 shard_map.115
  61.3 21.2 %all_to_all.32 = f32[256,2,128]{2,1,0:T(2,128)S(1)} all-to-all(f32[256,2,128]{2,1,0:T(2,128)S(1)} %bitcast.38), channel_id=1, replica_groups=mesh['ka'=32,'pa'=8] {'ka','pa'}, dimensions={0} | all-to-all | bytes 524288 | tf_op jit(solution)/shard_map/all_to_all | solution.py:266
  82.5 1.4 shard_map.116
  83.8 21.2 %all_to_all.33 = f32[256,2,128]{2,1,0:T(2,128)S(1)} all-to-all(f32[256,2,128]{2,1,0:T(2,128)S(1)} %bitcast.39), channel_id=1, replica_groups=mesh['ka'=32,'pa'=8] {'ka','pa'}, dimensions={0} | all-to-all | bytes 524288 | tf_op jit(solution)/shard_map/all_to_all | solution.py:266
  105.0 0.0 copy-start.4
  105.0 0.0 copy-start.5
  105.0 0.5 shard_map.117
  105.5 21.2 %all_to_all.34 = f32[256,2,128]{2,1,0:T(2,128)S(1)} all-to-all(f32[256,2,128]{2,1,0:T(2,128)S(1)} %bitcast.36), channel_id=1, replica_groups=mesh['ka'=32,'pa'=8] {'ka','pa'}, dimensions={0} | all-to-all | bytes 524288 | tf_op jit(solution)/shard_map/all_to_all | solution.py:266
  126.7 0.7 shard_map.118
  127.4 22.3 %all_to_all.35 = f32[8,2,32,256]{3,2,1,0:T(8,128)S(1)} all-to-all(f32[8,2,32,256]{3,2,1,0:T(8,128)S(1)} %shard_map.118), channel_id=1, replica_groups=mesh['ka'=32,'pa'=8] {'pa'}, dimensions={0} | all-to-all | bytes 1048576 | tf_op jit(solution)/shard_map/all_to_all | solution.py:282
  149.7 0.0 copy-done.4
  149.7 0.0 copy-done.5
  149.7 0.9 fusion.2
Async XLA Ops:
  2.3 58.4 %copy-start = (bf16[256,256]{1,0:T(8,128)(2,1)S(1)}, bf16[256,256]{1,0:T(8,128)(2,1)}, u32[]{:S(2)}) copy-start(bf16[256,256]{1,0:T(8,128)(2,1)} %constant.17.clone.back_low) | copy-start | bytes 393220
  2.4 58.4 %copy-start.1 = (bf16[256,256]{1,0:T(8,128)(2,1)S(1)}, bf16[256,256]{1,0:T(8,128)(2,1)}, u32[]{:S(2)}) copy-start(bf16[256,256]{1,0:T(8,128)(2,1)} %constant.16.clone.back_high) | copy-start | bytes 393220
  2.4 58.4 %copy-start.2 = (bf16[256,256]{1,0:T(8,128)(2,1)S(1)}, bf16[256,256]{1,0:T(8,128)(2,1)}, u32[]{:S(2)}) copy-start(bf16[256,256]{1,0:T(8,128)(2,1)} %constant.15.clone.rows_low) | copy-start | bytes 393220
  2.4 58.4 %copy-start.3 = (bf16[256,256]{1,0:T(8,128)(2,1)S(1)}, bf16[256,256]{1,0:T(8,128)(2,1)}, u32[]{:S(2)}) copy-start(bf16[256,256]{1,0:T(8,128)(2,1)} %constant.14.clone.rows_high) | copy-start | bytes 393220
  105.0 44.7 %copy-start.4 = (f32[8,256,32]{1,2,0:T(8,128)S(1)}, f32[8,256,32]{1,2,0:T(8,128)}, u32[]{:S(2)}) copy-start(f32[8,256,32]{1,2,0:T(8,128)} %param.11) | copy-start | bytes 786436
  105.0 44.7 %copy-start.5 = (f32[8,256,32]{1,2,0:T(8,128)S(1)}, f32[8,256,32]{1,2,0:T(8,128)}, u32[]{:S(2)}) copy-start(f32[8,256,32]{1,2,0:T(8,128)} %param.12) | copy-start | bytes 786436
